TPU v7x, 32 devices: a whole 2x2x4 slice. The times are simulated.
32 devices in a mesh: region: 1, drive: 16 (over z, y, core), street: 2 (over x).
Axes of the slice: x: 2, y: 2, z: 4, core: 2. Of those that a mesh axis runs over, the one named last changes fastest.
Arguments:
- pt_count: int32 [64], P(('region', 'drive')), may hold values from 16 to 256, as said below
- partner_dev: int32 [64, 4], P('region'), may hold values from 0 to 15, all different within a row; in each aligned block of 4 rows (0 to 3, 4 to 7, ...) at most 2 rows name the same one
- partner_pick: int32 [64, 4], P('region'), may hold values from 0 to 3
- knot_own: int32 [64, 256], P(('region', 'drive'), 'street'), may hold values from 0 to 508
- knot_partner: int32 [64, 256], P(('region', 'drive'), 'street'), may hold values from 0 to 508
- match_slot: int32 [64, 256], P(('region', 'drive'), 'street'), may hold values from 0 to 3
- spline: float32 [2, 64, 256], P(None, ('region', 'drive'), 'street'), may hold values from 0 to 1
- geometry: float32 [12, 64, 256], P(None, ('region', 'drive'), 'street'), may hold values from -6 to 6
- point_weight: float32 [64, 256], P(('region', 'drive'), 'street'), may hold values from 0.2 to 5
- point_resid: float32 [64, 256], P(('region', 'drive'), 'street'), may hold values from -6 to 6
Outputs:
- step: float32 [64, 8, 384], P(('region', 'drive'), 'street')
- cg_resid: float32 [64, 8, 384], P(('region', 'drive'), 'street')
Inputs may be any that keep to these rules, and one draw needn't show every extreme that they name: `pt_count`: some drive has exactly 256 live slots; slots at or beyond a drive's count are ignored. `partner_dev`: the 4 partners of a drive lie on different indices of drive. Among the drives of one index of drive (aligned blocks of 4 rows) at most 2 name any one index, a bound that some block reaches.
All inputs are finite; a program needn't handle non-finite values.
Results may differ from a plain program's by a relative error of at most 0.00011.
Values sent between devices are 32-bit elements; how exact they have to be, the bound alone decides.
No kernel may reach another device: no remote copies, remote signals or barrier semaphores. Data moves between devices by JAX's collectives and lax.ppermute only.
A program may use at most 64 MiB of HBM per device.

v0:
```python
import jax
import jax.numpy as jnp
from jax import lax
from jax.sharding import PartitionSpec as P

NBLK = 8
DOF = 6
PARAMS = 384
MATCH = 4
ITERS = 2


DAMPING = 1.0


def spline_basis(position):
    remain = 1.0 - position
    cube = position * position * position
    square = position * position
    return (
        jnp.stack(
            [
                remain * remain * remain,
                3.0 * cube - 6.0 * square + 4.0,
                -3.0 * cube + 3.0 * square + 3.0 * position + 1.0,
                cube,
            ]
        )
        / 6.0
    )


def point_coeffs(position, normals):
    basis = spline_basis(position)
    return (basis[:, None] * normals[None]).reshape((4 * DOF,) + normals.shape[1:])


def global_sums(values):
    return lax.psum((values[0],), ("drive", "street"))


def body(
    pt_count,
    partner_dev,
    partner_pick,
    knot_own,
    knot_partner,
    match_slot,
    spline,
    geometry,
    point_weight,
    point_resid,
):
    drive_count = knot_own.shape[0]
    point_share = knot_own.shape[1]
    drive_lanes = lax.axis_size("drive")
    param_width = NBLK * PARAMS
    capacity = min(drive_count, max(2, 2 * drive_count * MATCH // drive_lanes))
    slot_count = drive_lanes * capacity
    lane_index = lax.axis_index("drive")
    street_index = lax.axis_index("street")
    dest_all = partner_dev.reshape(drive_lanes, drive_count * MATCH)
    picks_all = partner_pick.reshape(drive_lanes, drive_count * MATCH)
    lane_ids = jnp.arange(drive_lanes, dtype=jnp.int32)
    one_hot = (dest_all[:, :, None] == lane_ids[None, None, :]).astype(jnp.int32)
    ranks_all = jnp.sum((jnp.cumsum(one_hot, axis=1) - one_hot) * one_hot, axis=2)
    matched = (dest_all == lane_index)[:, :, None] & (
        ranks_all[:, :, None] == jnp.arange(capacity, dtype=jnp.int32)[None, None, :]
    )
    filled = jnp.sum(matched.astype(jnp.int32), axis=1)
    served = jnp.sum(jnp.where(matched, picks_all[:, :, None], 0), axis=1) + drive_count * (
        1 - filled
    )
    served = served.reshape(slot_count)
    dest_mine = lax.dynamic_index_in_dim(dest_all, lane_index, 0, keepdims=False)
    ranks_mine = lax.dynamic_index_in_dim(ranks_all, lane_index, 0, keepdims=False)
    slot_of = (dest_mine * capacity + ranks_mine).reshape(drive_count, MATCH)
    slot_numbers = street_index * point_share + jnp.arange(point_share, dtype=jnp.int32)
    live = slot_numbers[None, :] < pt_count[:, None]
    weights = jnp.where(live, point_weight, jnp.zeros_like(point_weight))
    offsets = jnp.arange(4 * DOF, dtype=jnp.int32)[:, None, None]
    drive_base = (jnp.arange(drive_count, dtype=jnp.int32) * param_width)[None, :, None]
    own_index = drive_base + knot_own[None] * DOF + offsets
    row_of = jnp.sum(
        jnp.where(
            match_slot[:, :, None] == jnp.arange(MATCH, dtype=jnp.int32)[None, None, :],
            slot_of[:, None, :],
            0,
        ),
        axis=2,
    )
    partner_index = row_of[None] * param_width + knot_partner[None] * DOF + offsets
    coef_own = point_coeffs(spline[0], geometry[:DOF])
    coef_partner = point_coeffs(spline[1], geometry[DOF:])
    own_width = drive_count * param_width
    partner_width = slot_count * param_width

    def spread_terms(own_values, partner_values):
        own_terms = jax.ops.segment_sum(
            own_values.reshape(-1), own_index.reshape(-1), num_segments=own_width
        )
        partner_terms = jax.ops.segment_sum(
            partner_values.reshape(-1), partner_index.reshape(-1), num_segments=partner_width
        )
        return (own_terms, partner_terms)

    def fold_returned(returned):
        moved = jnp.moveaxis(returned, 1, 0)
        summed = jax.ops.segment_sum(moved, served, num_segments=drive_count + 1)[:drive_count]
        return jnp.moveaxis(summed, 0, 1)

    def collect_terms(own_terms, partner_terms):
        term_kinds = own_terms.shape[0]
        own_terms = own_terms.reshape(term_kinds, drive_count, NBLK, PARAMS)
        partner_terms = partner_terms.reshape(term_kinds, slot_count, NBLK, PARAMS)
        returned = lax.all_to_all(partner_terms, "drive", split_axis=1, concat_axis=1, tiled=True)
        return lax.psum_scatter(
            own_terms + fold_returned(returned), "street", scatter_dimension=2, tiled=True
        )

    weighted = weights * point_resid
    grad_own, grad_partner = spread_terms(-coef_own * weighted, coef_partner * weighted)
    diag_own, diag_partner = spread_terms(
        coef_own * coef_own * weights, coef_partner * coef_partner * weights
    )
    first = collect_terms(jnp.stack([grad_own, diag_own]), jnp.stack([grad_partner, diag_partner]))
    gradient = first[0]
    diagonal = DAMPING + first[1]
    solution = jnp.zeros_like(gradient)
    residual = gradient
    precond = residual / diagonal
    direction = precond
    inner_now = global_sums((jnp.sum(residual * precond),))[0]
    for iteration in range(ITERS):
        whole = lax.all_gather(direction, "street", axis=1, tiled=True)
        padded = jnp.concatenate([whole, jnp.zeros((1, NBLK, PARAMS), jnp.float32)], axis=0)
        outgoing = jnp.take(padded, served, axis=0)
        partner_whole = lax.all_to_all(outgoing, "drive", split_axis=0, concat_axis=0, tiled=True)
        own_flat = whole.reshape(-1)
        partner_flat = partner_whole.reshape(-1)
        projected = jnp.sum(coef_own * own_flat[own_index], axis=0) - jnp.sum(
            coef_partner * partner_flat[partner_index], axis=0
        )
        scaled = weights * projected
        hessian_own_terms, hessian_partner_terms = spread_terms(
            coef_own * scaled, -coef_partner * scaled
        )
        image = (
            DAMPING * direction
            + collect_terms(hessian_own_terms[None], hessian_partner_terms[None])[0]
        )
        step_size = inner_now / global_sums((jnp.sum(direction * image),))[0]
        solution = solution + step_size * direction
        residual = residual - step_size * image
        if iteration + 1 < ITERS:
            precond = residual / diagonal
            inner_next = global_sums((jnp.sum(residual * precond),))[0]
            direction = precond + inner_next / inner_now * direction
            inner_now = inner_next
    return (solution, residual)


def solution(mesh):
    placed = (
        P(("region", "drive")),
        P("region", None),
        P("region", None),
        P(("region", "drive"), "street"),
        P(("region", "drive"), "street"),
        P(("region", "drive"), "street"),
        P(None, ("region", "drive"), "street"),
        P(None, ("region", "drive"), "street"),
        P(("region", "drive"), "street"),
        P(("region", "drive"), "street"),
    )
    return jax.shard_map(
        body,
        mesh=mesh,
        in_specs=placed,
        out_specs=(P(("region", "drive"), "street", None), P(("region", "drive"), "street", None)),
        check_vma=False,
    )
```

profile of v0, /device:TPU:0, one launch (start us, length us, event | category | flops | bytes accessed | tf_op | source)
XLA Modules:
  0.0 1031.4 jit_solution(6730029601813028511)
XLA Ops:
  7.2 0.7 multiply_multiply_fusion.3
  7.9 0.7 copy-done.2
  9.6 0.6 copy-done.3
  10.3 0.6 copy-done.4
  11.0 0.6 copy-done.7
  11.8 64.6 %scatter_custom_fusion.2 = f32[98304]{0:T(1024)S(1)} fusion(s32[12288]{0:T(1024)S(1)} %bitcast.119, f32[12288]{0:T(1024)S(1)} %get-tuple-element.20, f32[]{:T(128)} %constant.27.clone.1), kind=kCustom, calls=%fused_computation.28 | custom fusion | flops 12288 | bytes 393220 | tf_op jit(solution)/shard_map/scatter-add | solution.py:102
  76.5 64.6 %scatter_custom_fusion.3 = f32[98304]{0:T(1024)S(1)} fusion(s32[12288]{0:T(1024)S(1)} %bitcast.120, f32[12288]{0:T(1024)S(1)} %get-tuple-element.19, f32[]{:T(128)} %constant.27.clone.1), kind=kCustom, calls=%fused_computation.26 | custom fusion | flops 12288 | bytes 393220 | tf_op jit(solution)/shard_map/scatter-add | solution.py:102
  141.2 0.9 pad_maximum_fusion
  142.1 7.4 all-to-all-start
  149.6 0.7 copy-done.5
  150.8 0.6 copy-done.6
  151.5 64.5 %scatter_custom_fusion = f32[12288]{0:T(1024)S(1)} fusion(s32[12288]{0:T(1024)S(1)} %bitcast.123, f32[12288]{0:T(1024)S(1)} %get-tuple-element.17, f32[]{:T(128)} %constant.27.clone.1), kind=kCustom, calls=%fused_computation.79 | custom fusion | flops 12288 | bytes 49156 | tf_op jit(solution)/shard_map/scatter-add | solution.py:99
  216.0 64.5 %scatter_custom_fusion.1 = f32[12288]{0:T(1024)S(1)} fusion(s32[12288]{0:T(1024)S(1)} %bitcast.124, f32[12288]{0:T(1024)S(1)} %get-tuple-element.18, f32[]{:T(128)} %constant.27.clone.1), kind=kCustom, calls=%fused_computation.77 | custom fusion | flops 12288 | bytes 49156 | tf_op jit(solution)/shard_map/scatter-add | solution.py:99
  280.6 0.6 copy-done.10
  282.5 2.1 scatter_fusion
  284.7 0.6 fusion.10
  285.4 22.6 %all-reduce.8.cloned.1.call-done = f32[2,4,8,384]{3,2,0,1:T(8,128)} async-done(((f32[2,4,8,384]{3,2,0,1:T(8,128)}), f32[2,4,8,384]{3,2,0,1:T(8,128)}) %all-reduce.8.cloned.1.call-update) | async-done | bytes 98320
  308.0 0.8 fusion.27
  308.8 4.5 all_gather.6
  313.3 0.6 gather_fusion.4
  313.9 0.8 broadcast_select_fusion.1
  314.8 5.6 all-to-all-start.1
  320.4 68.0 %gather_fusion = f32[12288]{0:T(1024)S(1)} fusion(f32[12288]{0:T(1024)S(1)} %reshape.357, s32[12288]{0:T(1024)S(1)} %broadcast_clamp_fusion.1), kind=kCustom, calls=%fused_computation.2 | custom fusion | bytes 147456 | tf_op jit(solution)/shard_map/gather | solution.py:141
  388.6 68.0 %gather_fusion.1 = f32[12288]{0:T(1024)S(1)} fusion(f32[98304]{0:T(1024)S(1)} %reshape.358, s32[12288]{0:T(1024)S(1)} %broadcast_clamp_fusion), kind=kCustom, calls=%fused_computation.3 | custom fusion | bytes 147456 | tf_op jit(solution)/shard_map/gather | solution.py:142
  456.7 64.6 %scatter_custom_fusion.6 = f32[98304]{0:T(1024)S(1)} fusion(s32[12288]{0:T(1024)S(1)} %bitcast.121, f32[12288]{0:T(1024)S(1)} %get-tuple-element.15, f32[]{:T(128)} %constant.27.clone.1), kind=kCustom, calls=%fused_computation.24 | custom fusion | flops 12288 | bytes 393220 | tf_op jit(solution)/shard_map/scatter-add | solution.py:102
  521.3 0.8 reshape_broadcast_in_dim.13
  522.1 6.0 all-to-all-start.2
  528.1 64.5 %scatter_custom_fusion.5 = f32[12288]{0:T(1024)S(1)} fusion(s32[12288]{0:T(1024)S(1)} %bitcast.125, f32[12288]{0:T(1024)S(1)} %get-tuple-element.16, f32[]{:T(128)} %constant.27.clone.1), kind=kCustom, calls=%fused_computation.75 | custom fusion | flops 12288 | bytes 49156 | tf_op jit(solution)/shard_map/scatter-add | solution.py:99
  592.7 1.8 scatter_fusion.1
  594.6 7.8 all-reduce.3
  602.4 0.6 multiply_reduce_fusion.2
  603.0 40.9 %all-reduce.5 = (f32[]{:T(128)}, f32[]{:T(128)}) all-reduce(f32[]{:T(128)} %get-tuple-element.4, f32[]{:T(128)} %get-tuple-element.3), channel_id=1, replica_groups=mesh['region'=1,'drive'=16,'street'=2] {'drive','street'}, use_global_device_ids=true, to_apply=%region_12.13 | all-reduce | flops 2 | bytes 16 | tf_op jit(solution)/shard_map/psum | solution.py:39
  645.3 0.6 multiply_reduce_fusion.1
  645.9 40.5 %psum.30 = f32[]{:T(128)} all-reduce(f32[]{:T(128)} %get-tuple-element.9), channel_id=1, replica_groups=mesh['region'=1,'drive'=16,'street'=2] {'drive','street'}, use_global_device_ids=true, to_apply=%region_22.24 | all-reduce | flops 1 | bytes 8 | tf_op jit(solution)/shard_map/psum | solution.py:39
  687.8 4.7 all_gather.7
  693.1 0.8 broadcast_select_fusion
  694.0 5.3 all-to-all-start.3
  699.3 68.0 %gather_fusion.2 = f32[12288]{0:T(1024)S(1)} fusion(f32[12288]{0:T(1024)S(1)} %reshape.359, s32[12288]{0:T(1024)S(1)} %broadcast_clamp_fusion.1), kind=kCustom, calls=%fused_computation.4 | custom fusion | bytes 147456 | tf_op jit(solution)/shard_map/gather | solution.py:141
  767.4 68.0 %gather_fusion.3 = f32[12288]{0:T(1024)S(1)} fusion(f32[98304]{0:T(1024)S(1)} %reshape.360, s32[12288]{0:T(1024)S(1)} %broadcast_clamp_fusion), kind=kCustom, calls=%fused_computation.5 | custom fusion | bytes 147456 | tf_op jit(solution)/shard_map/gather | solution.py:142
  835.5 64.6 %scatter_custom_fusion.9 = f32[98304]{0:T(1024)S(1)} fusion(s32[12288]{0:T(1024)S(1)} %bitcast.122, f32[12288]{0:T(1024)S(1)} %get-tuple-element.13, f32[]{:T(128)} %constant.27.clone.1), kind=kCustom, calls=%fused_computation.22 | custom fusion | flops 12288 | bytes 393220 | tf_op jit(solution)/shard_map/scatter-add | solution.py:102
  900.1 0.8 reshape_broadcast_in_dim.15
  901.0 6.0 all-to-all-start.4
  907.0 64.5 %scatter_custom_fusion.8 = f32[12288]{0:T(1024)S(1)} fusion(s32[12288]{0:T(1024)S(1)} %bitcast.126, f32[12288]{0:T(1024)S(1)} %get-tuple-element.14, f32[]{:T(128)} %constant.27.clone.1), kind=kCustom, calls=%fused_computation.73 | custom fusion | flops 12288 | bytes 49156 | tf_op jit(solution)/shard_map/scatter-add | solution.py:99
  971.5 1.8 scatter_fusion.2
  973.4 8.6 all-reduce.4
  982.0 0.6 multiply_reduce_fusion
  982.6 39.9 %psum.31 = f32[]{:T(128)} all-reduce(f32[]{:T(128)} %multiply_reduce_fusion), channel_id=1, replica_groups=mesh['region'=1,'drive'=16,'street'=2] {'drive','street'}, use_global_device_ids=true, to_apply=%region_30.32 | all-reduce | flops 1 | bytes 8 | tf_op jit(solution)/shard_map/psum | solution.py:39
  1023.9 0.7 multiply_subtract_fusion
  (92 shorter events, 3.9 us)
Async XLA Ops:
  7.2 0.7 copy-start.1
  7.9 0.7 copy-start.2
  9.5 0.7 copy-start.3
  10.2 0.7 copy-start.4
  10.9 0.7 copy-start.7
  10.9 0.7 copy-start.8
  11.0 0.7 copy-start.9
  142.1 140.4 %all-to-all-start = ((f32[2,32,8,384]{3,2,0,1:T(8,128)}), f32[2,32,8,384]{3,2,0,1:T(8,128)S(1)}, u32[]{:S(2)}, u32[]{:S(2)}) async-start(f32[2,32,8,384]{3,2,0,1:T(8,128)} %pad_maximum_fusion), calls=%async_computation | async-start | bytes 1572864 | tf_op jit(solution)/shard_map/all_to_all | solution.py:116
  149.5 158.5 %all-reduce.8.cloned.1.call-start = ((), (), s32[]{:S(2)}) async-start(), calls=%async_computation.5 | async-start | bytes 196608
  149.6 0.7 copy-start.5
  150.7 0.7 copy-start.6
  280.5 0.7 copy-start.10
  314.8 73.8 %all-to-all-start.1 = ((f32[32,8,384]{2,1,0:T(8,128)}), f32[32,8,384]{2,1,0:T(8,128)S(1)}, u32[]{:S(2)}, u32[]{:S(2)}) async-start(f32[32,8,384]{2,1,0:T(8,128)} %broadcast_select_fusion.1), calls=%async_computation.1 | async-start | bytes 786432 | tf_op jit(solution)/shard_map/all_to_all | solution.py:138
  522.1 70.5 %all-to-all-start.2 = ((f32[1,32,8,384]{3,2,0,1:T(8,128)}), f32[1,32,8,384]{3,2,0,1:T(8,128)S(1)}, u32[]{:S(2)}, u32[]{:S(2)}) async-start(f32[1,32,8,384]{3,2,0,1:T(8,128)} %reshape_broadcast_in_dim.13), calls=%async_computation.2 | async-start | bytes 786432 | tf_op jit(solution)/shard_map/all_to_all | solution.py:116
  594.5 7.8 copy-start
  694.0 73.4 %all-to-all-start.3 = ((f32[32,8,384]{2,1,0:T(8,128)}), f32[32,8,384]{2,1,0:T(8,128)S(1)}, u32[]{:S(2)}, u32[]{:S(2)}) async-start(f32[32,8,384]{2,1,0:T(8,128)} %broadcast_select_fusion), calls=%async_computation.3 | async-start | bytes 786432 | tf_op jit(solution)/shard_map/all_to_all | solution.py:138
  901.0 70.5 %all-to-all-start.4 = ((f32[1,32,8,384]{3,2,0,1:T(8,128)}), f32[1,32,8,384]{3,2,0,1:T(8,128)S(1)}, u32[]{:S(2)}, u32[]{:S(2)}) async-start(f32[1,32,8,384]{3,2,0,1:T(8,128)} %reshape_broadcast_in_dim.15), calls=%async_computation.4 | async-start | bytes 786432 | tf_op jit(solution)/shard_map/all_to_all | solution.py:116
Sparse Core Ops, SparseCore 0:
  285.5 22.4 all-reduce.7
where the time goes:
time: 1030 us
  other arithmetic  531 us (52%)
  local copies, waits for them, and re-layouts  281 us (27%)
  blocking collectives  147 us (14%)
  starting transfers between devices  30.3 us (3%)
  waiting for transfers between devices  22.6 us (2%)
  between operations  19.3 us (2%)
    scatter-add x4, other arithmetic, spread_terms(): jax.ops.segment_sum(partner_values.reshape(-1), partner_index.reshape(-1)...  258 us
    scatter-add x4, other arithmetic, spread_terms(): jax.ops.segment_sum(own_values.reshape(-1), own_index.reshape(-1), num_se...  258 us
    gather x2, local copies, waits for them, and re-layouts, body(): own_flat[own_index]  136 us
    gather x2, local copies, waits for them, and re-layouts, body(): partner_flat[partner_index]  136 us
    psum x3, blocking collectives, global_sums(): return lax.psum((values[0],), ('drive', 'street'))  121 us
    unnamed x2, waiting for transfers between devices  22.6 us
  transfers between devices with their start and end apart: 6, of which 1 were waited for; matrix products, arithmetic and copies ran while one was open for 38% of the time, Pallas kernels for 0%

commit v1 on v0

v1 whole, which is shorter than its diff:
```python
import jax
import jax.numpy as jnp
from jax import lax
from jax.experimental import pallas as pl
from jax.experimental.pallas import tpu as pltpu
from jax.sharding import PartitionSpec as P

NBLK = 8
DOF = 6
PARAMS = 384
MATCH = 4
LANES = 128
HIGH = 4
CAP = 2
SUB = 8
F32 = jnp.float32
BF16 = jnp.bfloat16


def iota(shape, dim):
    return lax.broadcasted_iota(jnp.int32, shape, dim)


def take_lanes(values, index):
    return jnp.take_along_axis(values, index, axis=1, mode="promise_in_bounds")


def row_of(block, row, count=SUB):
    return jnp.broadcast_to(block[row : row + 1, :], (count, LANES))


def basis_of(s):
    remain = 1.0 - s
    square = s * s
    cube = square * s
    return (
        remain * remain * remain * (1.0 / 6.0),
        (3.0 * cube - 6.0 * square + 4.0) * (1.0 / 6.0),
        (-3.0 * cube + 3.0 * square + 3.0 * s + 1.0) * (1.0 / 6.0),
        cube * (1.0 / 6.0),
    )


def split_two(values):
    high = values.astype(BF16)
    low = (values - high.astype(F32)).astype(BF16)
    return jnp.concatenate([high, low], axis=1)


def spread(knot, kinds):
    low = jnp.bitwise_and(knot, LANES - 1)
    high = jnp.right_shift(knot, 7)
    hot = jnp.where(iota((LANES, LANES), 0) == jnp.broadcast_to(low[0:1], (LANES, LANES)), 1.0, 0.0)
    hot = hot.astype(BF16)
    hot = jnp.concatenate([hot, hot], axis=1)
    high32 = jnp.broadcast_to(high[0:1], (4 * SUB, LANES))
    masks = []
    for h in range(HIGH):
        mask = jnp.where(high32 == h, 1.0, 0.0).astype(BF16)
        masks.append(jnp.concatenate([mask, mask], axis=1))
    rows = []
    for kind in kinds:
        parts = split_two(jnp.concatenate(kind, axis=0))
        for h in range(HIGH):
            rows.append(parts * masks[h])
    left = jnp.concatenate(rows, axis=0)
    return lax.dot_general(left, hot, (((1,), (1,)), ((), ())), preferred_element_type=F32)


def fold_shifts(acc, base):
    lane = iota((SUB, LANES), 1)
    out = []
    before = None
    for h in range(HIGH):
        tiles = [acc[base + h * 32 + k * SUB : base + h * 32 + (k + 1) * SUB, :] for k in range(4)]
        rolled = [None] + [pltpu.roll(tiles[k], k, axis=1) for k in range(1, 4)]
        total = tiles[0]
        for k in range(1, 4):
            other = before[k] if before is not None else jnp.zeros((SUB, LANES), F32)
            total = total + jnp.where(lane >= k, rolled[k], other)
        out.append(total)
        before = rolled
    return out


def gather_value(tiles, knot, basis, normals):
    total = None
    for k in range(4):
        index = knot + k
        low = jnp.bitwise_and(index, LANES - 1)
        high = jnp.right_shift(index, 7)
        value = take_lanes(tiles[HIGH - 1], low)
        for h in range(HIGH - 1):
            value = jnp.where(high == h, take_lanes(tiles[h], low), value)
        term = basis[k] * value
        total = term if total is None else total + term
    return jnp.sum(normals * total, axis=0, keepdims=True)


def own_tile(own_ref, h, a):
    normals = own_ref[h, a, 0:SUB, :]
    info = own_ref[h, a, SUB : 2 * SUB, :]
    return normals, row_of(info, 0).astype(jnp.int32), basis_of(row_of(info, 1)), row_of(info, 2)


def inc_tile(inc_ref, block, rank):
    normals = inc_ref[block, pl.ds(pl.multiple_of(rank * SUB, SUB), SUB), :]
    info = inc_ref[block, 2 * SUB : 3 * SUB, :]
    info = jnp.where(rank == 0, info, jnp.concatenate([info[4:8], info[0:4]], axis=0))
    return normals, row_of(info, 0).astype(jnp.int32), basis_of(row_of(info, 1)), row_of(info, 2)


def decode(code, street_size):
    pick = jnp.bitwise_and(code, 3)
    tile = jnp.right_shift(code, 2)
    rank = jnp.bitwise_and(tile, 1)
    block = jnp.right_shift(tile, 1)
    lane = lax.div(block, street_size)
    part = block - lane * street_size
    return pick, rank, block, lane, part


def send_kernel(
    meta, counts, dev, picks, knot_own, knot_par, match, spline, geometry, weight, resid,
    send, own, tab, filled, taken, normals_s, info_s, match_s,
):
    drives = counts.shape[0]
    lanes = send.shape[0]
    street_size = send.shape[1]
    lane = meta[0]
    street = meta[1]
    for j in range(lanes):
        taken[j] = 0
        filled[2 * j] = -1
        filled[2 * j + 1] = -1
    for a in range(drives):
        for m in range(MATCH):
            e = a * MATCH + m
            dest = dev[lane * drives + a, m]
            rank = taken[dest]
            taken[dest] = rank + 1
            tab[e] = dest
            tab[drives * MATCH + e] = rank
            filled[2 * dest + rank] = e
    slot = street * LANES + iota((1, LANES), 1)
    zero1 = jnp.zeros((1, LANES), F32)
    for a in range(drives):
        w = jnp.where(slot < counts[a], weight[a : a + 1, :], 0.0)
        root = jnp.sqrt(w)
        rho = -(root * resid[a : a + 1, :])
        own[a, 0:SUB, :] = jnp.concatenate(
            [geometry[d, a : a + 1, :] * root for d in range(DOF)] + [zero1] * 2, axis=0
        )
        own[a, SUB : 2 * SUB, :] = jnp.concatenate(
            [knot_own[a : a + 1, :].astype(F32), spline[0, a : a + 1, :], rho] + [zero1] * 5, axis=0
        )
        normals_s[a] = jnp.concatenate(
            [-(geometry[DOF + d, a : a + 1, :] * root) for d in range(DOF)] + [zero1] * 2, axis=0
        )
        half = [knot_par[a : a + 1, :].astype(F32), spline[1, a : a + 1, :], rho, zero1]
        info_s[a] = jnp.concatenate(half + half, axis=0)
        match_s[a] = jnp.broadcast_to(match[a : a + 1, :], (SUB, LANES))
    row = iota((SUB, LANES), 0)
    for j in range(lanes):
        normals = []
        infos = []
        flags = []
        for r in range(CAP):
            e = filled[2 * j + r]
            safe = jnp.maximum(e, 0)
            a = jnp.right_shift(safe, 2)
            m = jnp.where(e < 0, -1, jnp.bitwise_and(safe, 3))
            pick = picks[lane * drives + a, jnp.bitwise_and(safe, 3)]
            there = jnp.logical_and(e >= 0, counts[a] > street * LANES)
            flags.append(jnp.where(there, pick + 1, 0).astype(F32))
            normals.append(jnp.where(match_s[a] == m, normals_s[a], 0.0))
            infos.append(info_s[a])
        info = jnp.where(row < 4, infos[0], infos[1])
        info = jnp.where(row == 3, flags[0], jnp.where(row == 7, flags[1], info))
        for t in range(street_size):
            send[j, t, 0:SUB, :] = normals[0]
            send[j, t, SUB : 2 * SUB, :] = normals[1]
            send[j, t, 2 * SUB : 3 * SUB, :] = info


def put_values(out_ref, tab, own_ref, inc_ref, lst, tiles_ref):
    street_size, drives = own_ref.shape[0], own_ref.shape[1]
    entries = drives * MATCH
    for a in range(drives):
        tiles = [tiles_ref[a, h] for h in range(HIGH)]
        for s in range(street_size):
            normals, knot, basis, _ = own_tile(own_ref, s, a)
            value = gather_value(tiles, knot, basis, normals)
            for m in range(MATCH):
                e = a * MATCH + m
                out_ref[tab[e], pl.ds(tab[entries + e] * street_size + s, 1), :] = value

    def one(code):
        pick, rank, block, lane, part = decode(code, street_size)
        normals, knot, basis, _ = inc_tile(inc_ref, block, rank)
        value = gather_value([tiles_ref[pick, h] for h in range(HIGH)], knot, basis, normals)
        out_ref[lane, pl.ds((CAP + rank) * street_size + part, 1), :] = value

    count = lst[lst.shape[0] - 1]

    def two(i, carry):
        one(lst[2 * i])
        one(lst[2 * i + 1])
        return carry

    lax.fori_loop(0, jnp.right_shift(count + 1, 1), two, 0)


def own_sum(sent, got, tab, a, s, street_size, entries):
    e = a * MATCH
    total = sent[tab[e], pl.ds(tab[entries + e] * street_size + s, 1), :]
    for m in range(MATCH):
        e = a * MATCH + m
        total = total + got[tab[e], pl.ds((CAP + tab[entries + e]) * street_size + s, 1), :]
    return total


def inc_sum(sent, got, rank, lane, part, street_size):
    return (
        got[lane, pl.ds(rank * street_size + part, 1), :]
        + sent[lane, pl.ds((CAP + rank) * street_size + part, 1), :]
    )


def spread_all(acc, own_ref, inc_ref, lst, kinds_own, kinds_inc):
    street_size, drives = own_ref.shape[0], own_ref.shape[1]
    for a in range(drives):
        total = None
        for s in range(street_size):
            normals, knot, basis, rho = own_tile(own_ref, s, a)
            coeffs = [basis[k] * normals for k in range(4)]
            part = spread(knot, kinds_own(coeffs, rho, a, s))
            total = part if total is None else total + part
        acc[a] = total

    count = lst[lst.shape[0] - 1]

    def one(index):
        pick, rank, block, lane, part = decode(lst[index], street_size)
        normals, knot, basis, rho = inc_tile(inc_ref, block, rank)
        normals = jnp.where(index < count, normals, 0.0)
        coeffs = [basis[k] * normals for k in range(4)]
        return pick, spread(knot, kinds_inc(coeffs, rho, rank, lane, part))

    def two(i, carry):
        first = one(2 * i)
        second = one(2 * i + 1)
        for pick, value in (first, second):
            acc[pick] = acc[pick] + value
        return carry

    lax.fori_loop(0, jnp.right_shift(count + 1, 1), two, 0)


def start_kernel(tab, own, inc, grad, diag, direction, out, lst, acc):
    drives = own.shape[1]
    blocks = inc.shape[0]
    count = 0
    for b in range(blocks):
        flags = inc[b, 2 * SUB : 3 * SUB, :].astype(jnp.int32)
        for r in range(CAP):
            flag = flags[4 * r + 3, 0]
            lst[count] = (b * CAP + r) * 4 + flag - 1
            count = count + jnp.where(flag > 0, 1, 0)
    lst[count] = lst[jnp.maximum(count - 1, 0)]
    lst[lst.shape[0] - 1] = count

    def kinds(coeffs, rho, *_):
        return [[c * rho for c in coeffs], [c * c for c in coeffs]]

    spread_all(acc, own, inc, lst, kinds, kinds)
    for a in range(drives):
        sums = acc[a]
        gradient = fold_shifts(sums, 0)
        squares = fold_shifts(sums, 128)
        for h in range(HIGH):
            diagonal = 1.0 + squares[h]
            grad[a, h] = gradient[h]
            diag[a, h] = diagonal
            direction[a, h] = gradient[h] / diagonal
    out[...] = jnp.zeros(out.shape, F32)
    put_values(out, tab, own, inc, lst, direction)


def scalar_row(values):
    lane = iota((1, LANES), 1)
    row = jnp.zeros((1, LANES), F32)
    for i, value in enumerate(values):
        total = jnp.sum(jnp.sum(value, axis=0, keepdims=True), axis=1, keepdims=True)
        row = jnp.where(lane == i, total, row)
    return row


def pick_lane(row, i):
    return jnp.sum(jnp.where(iota((1, LANES), 1) == i, row, 0.0), axis=1, keepdims=True)


def middle_kernel(
    tab, lst, own, inc, grad, diag, direction, sent, got, image, values, out, acc, ratio
):
    street_size, drives = own.shape[0], own.shape[1]
    entries = drives * MATCH
    for a in range(drives):
        for s in range(street_size):
            values[pl.ds(s * drives + a, 1), :] = own_sum(sent, got, tab, a, s, street_size, entries)

    def kinds_own(coeffs, rho, a, s):
        value = jnp.broadcast_to(values[pl.ds(s * drives + a, 1), :], (SUB, LANES))
        return [[c * value for c in coeffs]]

    def kinds_inc(coeffs, rho, rank, lane, part):
        value = inc_sum(sent, got, rank, lane, part, street_size)
        value = jnp.broadcast_to(value, (SUB, LANES))
        return [[c * value for c in coeffs]]

    spread_all(acc, own, inc, lst, kinds_own, kinds_inc)
    first = jnp.zeros((SUB, LANES), F32)
    second = jnp.zeros((SUB, LANES), F32)
    for a in range(drives):
        sums = fold_shifts(acc[a], 0)
        for h in range(HIGH):
            p = direction[a, h]
            q = p + sums[h]
            image[a, h] = q
            ratio[a, h] = q / diag[a, h]
            first = first + grad[a, h] * p
            second = second + p * q
    out[...] = jnp.zeros(out.shape, F32)
    put_values(out, tab, own, inc, lst, ratio)
    row = scalar_row([first, second])
    rows = 2 * CAP * street_size
    for j in range(out.shape[0]):
        out[j, rows : rows + 1, :] = row


def dots_kernel(tab, grad, diag, direction, image, values, sent, got, resid, precond, steps, out):
    drives = grad.shape[0]
    street_size = values.shape[0] // drives
    entries = drives * MATCH
    rows = 2 * CAP * street_size
    total = got[0, rows : rows + 1, :]
    for j in range(1, got.shape[0]):
        total = total + got[j, rows : rows + 1, :]
    inner = pick_lane(total, 0)
    curve = pick_lane(total, 1)
    alpha = inner / curve
    one = jnp.zeros((SUB, LANES), F32)
    two = jnp.zeros((SUB, LANES), F32)
    three = jnp.zeros((SUB, LANES), F32)
    for a in range(drives):
        for h in range(HIGH):
            r = grad[a, h] - alpha * image[a, h]
            z = r / diag[a, h]
            resid[a, h] = r
            precond[a, h] = z
            one = one + r * z
            two = two + z * z
            three = three + z * direction[a, h]
    slots2 = jnp.zeros((1, LANES), F32)
    slots3 = jnp.zeros((1, LANES), F32)
    for a in range(drives):
        for s in range(street_size):
            before = values[pl.ds(s * drives + a, 1), :]
            value = before - alpha * own_sum(sent, got, tab, a, s, street_size, entries)
            slots2 = slots2 + value * value
            slots3 = slots3 + value * before
    head = iota((SUB, LANES), 0) == 0
    two = two + jnp.where(head, jnp.broadcast_to(slots2, (SUB, LANES)), 0.0)
    three = three + jnp.where(head, jnp.broadcast_to(slots3, (SUB, LANES)), 0.0)
    row = jnp.broadcast_to(scalar_row([one, two, three]), (SUB, LANES))
    for j in range(out.shape[0]):
        out[j] = row
    lane = iota((SUB, LANES), 1)
    steps[...] = jnp.where(lane == 0, alpha, jnp.where(lane == 1, inner, curve))


def last_kernel(
    meta, tab, lst, own, inc, direction, image, values, sent, got, sent2, got2, resid, precond,
    steps, o_p, o_z, o_r, o_h, o_q, acc, hess,
):
    street_size, drives = own.shape[0], own.shape[1]
    entries = drives * MATCH
    alpha = steps[0:1, 0:1]

    def kinds_own(coeffs, rho, a, s):
        value = values[pl.ds(s * drives + a, 1), :] - alpha * own_sum(
            sent2, got2, tab, a, s, street_size, entries
        )
        value = jnp.broadcast_to(value, (SUB, LANES))
        return [[c * value for c in coeffs]]

    def kinds_inc(coeffs, rho, rank, lane, part):
        value = inc_sum(sent, got, rank, lane, part, street_size) - alpha * inc_sum(
            sent2, got2, rank, lane, part, street_size
        )
        value = jnp.broadcast_to(value, (SUB, LANES))
        return [[c * value for c in coeffs]]

    spread_all(acc, own, inc, lst, kinds_own, kinds_inc)
    for a in range(drives):
        sums = fold_shifts(acc[a], 0)
        for h in range(HIGH):
            hess[a, h] = precond[a, h] + sums[h]
    blocks = o_p.shape[1]
    tiles = PARAMS // LANES
    row = iota((SUB, LANES), 0)
    points = []
    masks = []
    for q in range(tiles):
        entry = q * LANES + iota((SUB, LANES), 1)
        point = jnp.right_shift(entry * 10923, 16)
        points.append(point)
        masks.append(row == entry - point * DOF)
    for bl in range(blocks):
        block = meta[1] * blocks + bl
        high = jnp.right_shift(block, 1)
        offset = jnp.bitwise_and(block, 1) * (LANES // 2)
        indices = [offset + points[q] for q in range(tiles)]
        for a in range(drives):
            for source, target in (
                (direction, o_p), (precond, o_z), (resid, o_r), (hess, o_h), (image, o_q)
            ):
                tile = source[a, high]
                for q in range(tiles):
                    value = jnp.where(masks[q], take_lanes(tile, indices[q]), 0.0)
                    target[a, bl : bl + 1, q * LANES : (q + 1) * LANES] = jnp.sum(
                        value, axis=0, keepdims=True
                    )


def finish_kernel(steps, got, o_p, o_z, o_r, o_h, o_q, step_out, resid_out):
    total = got[0]
    for j in range(1, got.shape[0]):
        total = total + got[j]
    total = total[0:1, :]
    inner_next = pick_lane(total, 0)
    alpha = steps[0:1, 0:1]
    inner = steps[0:1, 1:2]
    curve = steps[0:1, 2:3]
    beta = inner_next / inner
    denominator = pick_lane(total, 1) + 2.0 * beta * pick_lane(total, 2) + beta * beta * curve
    last = inner_next / denominator
    for a in range(o_p.shape[0]):
        p = o_p[a]
        step_out[a] = alpha * p + last * (o_z[a] + beta * p)
        resid_out[a] = o_r[a] - last * (o_h[a] + beta * o_q[a])


def call(kernel, shapes, spaces_in, spaces_out, scratch=(), **kwargs):
    where = {"s": pltpu.SMEM, "v": pltpu.VMEM}
    return pl.pallas_call(
        kernel,
        out_shape=[jax.ShapeDtypeStruct(s, d) for s, d in shapes],
        in_specs=[pl.BlockSpec(memory_space=where[c]) for c in spaces_in],
        out_specs=[pl.BlockSpec(memory_space=where[c]) for c in spaces_out],
        scratch_shapes=list(scratch),
        compiler_params=pltpu.CompilerParams(vmem_limit_bytes=40 * 1024 * 1024),
        **kwargs,
    )


def body(
    pt_count,
    partner_dev,
    partner_pick,
    knot_own,
    knot_partner,
    match_slot,
    spline,
    geometry,
    point_weight,
    point_resid,
):
    drives = knot_own.shape[0]
    lanes = lax.axis_size("drive")
    street_size = lax.axis_size("street")
    meta = jnp.stack([lax.axis_index("drive"), lax.axis_index("street")]).astype(jnp.int32)
    entries = drives * MATCH
    blocks = lanes * street_size
    param = ((drives, HIGH, SUB, LANES), F32)
    send, mine, tab = call(
        send_kernel,
        [
            ((lanes, street_size, 3 * SUB, LANES), F32),
            ((drives, 2 * SUB, LANES), F32),
            ((2 * entries,), jnp.int32),
        ],
        "ssssvvvvvvv",
        "vvs",
        [
            pltpu.SMEM((CAP * lanes,), jnp.int32),
            pltpu.SMEM((lanes,), jnp.int32),
            pltpu.VMEM((drives, SUB, LANES), F32),
            pltpu.VMEM((drives, SUB, LANES), F32),
            pltpu.VMEM((drives, SUB, LANES), jnp.int32),
        ],
        name="send",
    )(
        meta, pt_count, partner_dev, partner_pick, knot_own, knot_partner, match_slot,
        spline, geometry, point_weight, point_resid,
    )
    if street_size == 2:
        peer = lax.ppermute(mine, "street", [(0, 1), (1, 0)])
        first = meta[1] == 0
        own = jnp.stack([jnp.where(first, mine, peer), jnp.where(first, peer, mine)])
    else:
        own = lax.all_gather(mine, "street", axis=0, tiled=False)
    inc = lax.all_to_all(
        send.reshape(blocks, 3 * SUB, LANES), ("drive", "street"), split_axis=0, concat_axis=0, tiled=True
    )
    exchange = ((lanes, 2 * CAP * street_size, LANES), F32)
    exchange2 = ((lanes, 2 * CAP * street_size + SUB, LANES), F32)
    acc = pltpu.VMEM((drives, 128, LANES), F32)
    list_size = CAP * blocks + 2
    grad, diag, direction, sent, lst = call(
        start_kernel,
        [param, param, param, exchange, ((list_size,), jnp.int32)],
        "svv",
        "vvvvs",
        [pltpu.VMEM((drives, 256, LANES), F32)],
        name="start",
    )(tab, own, inc)
    got = lax.all_to_all(sent, "drive", split_axis=0, concat_axis=0, tiled=True)
    image, values, sent2 = call(
        middle_kernel,
        [param, ((street_size * drives, LANES), F32), exchange2],
        "ssvvvvvvv",
        "vvv",
        [acc, pltpu.VMEM(param[0], F32)],
        name="middle",
    )(tab, lst, own, inc, grad, diag, direction, sent, got)
    got2 = lax.all_to_all(sent2, "drive", split_axis=0, concat_axis=0, tiled=True)
    resid, precond, steps, sent3 = call(
        dots_kernel,
        [param, param, ((SUB, LANES), F32), ((lanes, SUB, LANES), F32)],
        "svvvvvvv",
        "vvvv",
        name="dots",
    )(tab, grad, diag, direction, image, values, sent2, got2)
    got3 = lax.all_to_all(sent3, "drive", split_axis=0, concat_axis=0, tiled=True)
    shape = ((drives, NBLK // street_size, PARAMS), F32)
    parts = call(
        last_kernel,
        [shape] * 5,
        "sssvvvvvvvvvvvv",
        "vvvvv",
        [acc, pltpu.VMEM(param[0], F32)],
        name="last",
        cost_estimate=pl.CostEstimate(flops=200000000, bytes_accessed=8000000, transcendentals=0),
    )(meta, tab, lst, own, inc, direction, image, values, sent, got, sent2, got2, resid, precond, steps)
    return tuple(
        call(finish_kernel, [shape, shape], "vvvvvvv", "vv", name="finish")(steps, got3, *parts)
    )


def solution(mesh):
    placed = (
        P(("region", "drive")),
        P("region", None),
        P("region", None),
        P(("region", "drive"), "street"),
        P(("region", "drive"), "street"),
        P(("region", "drive"), "street"),
        P(None, ("region", "drive"), "street"),
        P(None, ("region", "drive"), "street"),
        P(("region", "drive"), "street"),
        P(("region", "drive"), "street"),
    )
    return jax.shard_map(
        body,
        mesh=mesh,
        in_specs=placed,
        out_specs=(P(("region", "drive"), "street", None), P(("region", "drive"), "street", None)),
        check_vma=False,
    )
```

time: 1030 us -> 76.7 us (0.07)
  other arithmetic: 531 us -> 0.09 us
  local copies, waits for them, and re-layouts: 281 us -> 2.07 us
  blocking collectives: 147 us -> 27.1 us
  Pallas kernels: 0 us -> 19.1 us
  between operations: 19.3 us -> 0.73 us
  starting transfers between devices: 30.3 us -> 12.6 us
    scatter-add x11 -> x0, other arithmetic: 522 us -> none  [the longest x4 258 us: spread_terms(): jax.ops.segment_sum(partner_values.reshape(-1), partner_index.reshape(-1)...]
    gather x6 -> x0, local copies, waits for them, and re-layouts: 273 us -> none  [the longest x2 136 us: body(): own_flat[own_index]]
    psum x3 -> x0, blocking collectives: 121 us -> none  [global_sums(): return lax.psum((values[0],), ('drive', 'street'))]
    all_to_all x0 -> x2, blocking collectives: none -> 27.1 us  [the longest x1 13.8 us: body(): got = lax.all_to_all(sent, 'drive', split_axis=0, concat_axis=0, tiled=True)]
    unnamed x2 -> x0, waiting for transfers between devices: 22.6 us -> none
    all_to_all x5 -> x2, starting transfers between devices: 30.3 us -> 10.8 us  [the longest x1 7.3 us: body(): lax.all_to_all(send.reshape(blocks, 3 * SUB, LANES), ('drive', 'street'),...]
    pallas_call x0 -> x6, Pallas kernels: none -> 19.1 us  [the longest x1 5.82 us: body(): call(start_kernel, [param, param, param, exchange, ((list_size,), jnp.int...]
    unnamed x2 -> x0, blocking collectives: 16.4 us -> none
  transfers between devices with their start and end apart: 6 -> 3, of which waited for: 1 -> 3; matrix products, arithmetic and copies ran while one was open for 38% -> 0% of each run, Pallas kernels for 0% -> 5%
where the time goes in v1:
time: 76.7 us; the launch traced here: 75.8 us
  blocking collectives  27.1 us (35%)
  Pallas kernels  19.1 us (25%)
  waiting for transfers between devices  14.1 us (18%)
  starting transfers between devices  12.6 us (16%)
  local copies, waits for them, and re-layouts  2.07 us (3%)
    all_to_all x1, blocking collectives, body(): got = lax.all_to_all(sent, 'drive', split_axis=0, concat_axis=0, tiled=True)  13.8 us
    all_to_all x1, blocking collectives, body(): lax.all_to_all(sent2, 'drive', split_axis=0, concat_axis=0, tiled=True)  13.4 us
    all_to_all x1, waiting for transfers between devices, body(): lax.all_to_all(send.reshape(blocks, 3 * SUB, LANES), ('drive', 'street'),...  7.32 us
    all_to_all x1, starting transfers between devices, body(): lax.all_to_all(send.reshape(blocks, 3 * SUB, LANES), ('drive', 'street'),...  7.3 us
    pallas_call x1, Pallas kernels, body(): call(start_kernel, [param, param, param, exchange, ((list_size,), jnp.int...  5.82 us
    pallas_call x1, Pallas kernels, body(): call(middle_kernel, [param, ((street_size * drives, LANES), F32), exchang...  4.69 us
    pallas_call x1, Pallas kernels, body(): call(last_kernel, [shape] * 5, 'sssvvvvvvvvvvvv', 'vvvvv', [acc, pltpu.VM...  3.68 us
    ppermute x1, waiting for transfers between devices, body(): peer = lax.ppermute(mine, 'street', [(0, 1), (1, 0)])  3.58 us
  transfers between devices with their start and end apart: 3, of which 3 were waited for; matrix products, arithmetic and copies ran while one was open for 0% of the time, Pallas kernels for 5%

profile of v1, /device:TPU:0, one launch (start us, length us, event | category | flops | bytes accessed | tf_op | source)
XLA Modules:
  0.0 75.8 jit_solution(3259453807002802539)
XLA Ops:
  0.6 0.0 copy-start.8
  0.6 0.7 copy-done.8
  1.3 0.0 copy-start.9
  1.3 0.1 copy.12.dev
  1.4 0.6 copy-done.9
  2.0 0.0 copy-start
  2.0 0.0 copy-start.2
  2.0 0.0 copy-start.3
  2.0 0.0 copy-start.4
  2.0 0.0 copy-start.5
  2.0 0.0 copy-start.6
  2.0 0.1 copy.13.picks
  2.1 0.0 copy-start.1
  2.1 0.0 copy-start.7
  2.1 0.1 pad_add_fusion.meta
  2.2 0.5 copy-done
  2.7 0.0 copy-done.2
  2.7 0.0 copy-done.3
  2.7 0.0 copy-done.4
  2.7 0.0 copy-done.5
  2.8 0.0 copy-done.6
  2.8 0.1 copy-done.1
  2.8 0.0 copy-done.7
  2.8 2.7 %send.1 = (f32[16,2,24,128]{3,2,1,0:T(8,128)}, f32[4,16,128]{2,1,0:T(8,128)S(1)}, s32[32]{0:T(128)S(1)}) custom-call(s32[2]{0:T(128)S(1)} %pad_add_fusion.meta, s32[4]{0:T(128)S(1)} %copy-done.7, s32[64,4]{1,0:T(8,128)S(1)} %copy.12.dev, s32[64,4]{1,0:T(8,128)S(1)} %copy.13.picks, s32[4,128]{1,0:T(4,128)S(1)} %copy-done.2, s32[4,128]{1,0:T(4,128)S(1)} %copy-done.3, ...), custom_call_target="tpu_custom_call" | custom-call | tf_op jit(solution)/shard_map/send/pallas_call | solution.py:486
  5.5 7.3 %all-to-all-start = ((f32[32,24,128]{2,1,0:T(8,128)}), f32[32,24,128]{2,1,0:T(8,128)S(1)}, u32[]{:S(2)}, u32[]{:S(2)}) async-start(f32[32,24,128]{2,1,0:T(8,128)} %bitcast.4), calls=%async_computation | async-start | bytes 786432 | tf_op jit(solution)/shard_map/all_to_all | solution.py:513
  12.9 1.8 %collective-permute-start = (f32[4,16,128]{2,1,0:T(8,128)S(1)}, f32[4,16,128]{2,1,0:T(8,128)S(1)}, u32[]{:S(2)}, u32[]{:S(2)}) collective-permute-start(f32[4,16,128]{2,1,0:T(8,128)S(1)} %get-tuple-element.23), channel_id=1, source_target_pairs={{0,1},{1,0},{2,3},{3,2},{4,5},{5,4},{6,7},{7,6},{8,9},{9,8},{10,11... | collective-permute-start | bytes 98312 | tf_op jit(solution)/shard_map/ppermute | solution.py:508
  14.7 3.6 %collective-permute-done = f32[4,16,128]{2,1,0:T(8,128)S(1)} collective-permute-done((f32[4,16,128]{2,1,0:T(8,128)S(1)}, f32[4,16,128]{2,1,0:T(8,128)S(1)}, u32[]{:S(2)}, u32[]{:S(2)}) %collective-permute-start) | collective-permute-done | bytes 32800 | tf_op jit(solution)/shard_map/ppermute | solution.py:508
  18.3 7.3 %all-to-all-done.inc = f32[32,24,128]{2,1,0:T(8,128)S(1)} async-done(((f32[32,24,128]{2,1,0:T(8,128)}), f32[32,24,128]{2,1,0:T(8,128)S(1)}, u32[]{:S(2)}, u32[]{:S(2)}) %all-to-all-start) | async-done | bytes 393248 | tf_op jit(solution)/shard_map/all_to_all | solution.py:513
  25.6 5.8 %start.1 = (f32[4,4,8,128]{3,2,1,0:T(8,128)S(1)}, f32[4,4,8,128]{3,2,1,0:T(8,128)S(1)}, f32[4,4,8,128]{3,2,1,0:T(8,128)S(1)}, f32[16,8,128]{2,1,0:T(8,128)S(1)}, s32[66]{0:T(128)S(1)}) custom-call(s32[32]{0:T(128)S(1)} %get-tuple-element.22.tab, f32[2,4,16,128]{3,2,1,0:T(8,128)S(1)} %pad_maximum_fusion.own, f32[32,24,128]{2,1,0:T(8,128)S(1)} %all-to-all-done.inc), custom_call_target="tpu_custom_call" | custom-call | tf_op jit(solution)/shard_map/start/pallas_call | solution.py:520
  31.4 13.8 %all_to_all.20.got = f32[16,8,128]{2,1,0:T(8,128)S(1)} all-to-all(f32[16,8,128]{2,1,0:T(8,128)S(1)} %get-tuple-element.29.sent), channel_id=1, replica_groups=mesh['region'=1,'drive'=16,'street'=2] {'drive'}, dimensions={0} | all-to-all | bytes 131072 | tf_op jit(solution)/shard_map/all_to_all | solution.py:528
  45.2 4.7 %middle.1 = (f32[4,4,8,128]{3,2,1,0:T(8,128)S(1)}, f32[8,128]{1,0:T(8,128)S(1)}, f32[16,16,128]{2,1,0:T(8,128)S(1)}) custom-call(s32[32]{0:T(128)S(1)} %get-tuple-element.22.tab, s32[66]{0:T(128)S(1)} %get-tuple-element.28.lst, f32[2,4,16,128]{3,2,1,0:T(8,128)S(1)} %pad_maximum_fusion.own, f32[32,24,128]{2,1,0:T(8,128)S(1)} %all-to-all-done.inc, ...), custom_call_target="tpu_custom_call" | custom-call | tf_op jit(solution)/shard_map/middle/pallas_call | solution.py:529
  49.9 13.4 %all_to_all.21.got.got2 = f32[16,16,128]{2,1,0:T(8,128)S(1)} all-to-all(f32[16,16,128]{2,1,0:T(8,128)S(1)} %get-tuple-element.32.sent.sent2), channel_id=1, replica_groups=mesh['region'=1,'drive'=16,'street'=2] {'drive'}, dimensions={0} | all-to-all | bytes 262144 | tf_op jit(solution)/shard_map/all_to_all | solution.py:537
  63.3 1.4 %dots.1 = (f32[4,4,8,128]{3,2,1,0:T(8,128)S(1)}, f32[4,4,8,128]{3,2,1,0:T(8,128)S(1)}, f32[8,128]{1,0:T(8,128)S(1)}, f32[16,8,128]{2,1,0:T(8,128)}) custom-call(s32[32]{0:T(128)S(1)} %get-tuple-element.22.tab, f32[4,4,8,128]{3,2,1,0:T(8,128)S(1)} %get-tuple-element.25.grad, f32[4,4,8,128]{3,2,1,0:T(8,128)S(1)} %get-tuple-element.26.diag, ...), custom_call_target="tpu_custom_call" | custom-call | tf_op jit(solution)/shard_map/dots/pallas_call | solution.py:538
  64.6 3.5 %all-to-all-start.3 = ((f32[16,8,128]{2,1,0:T(8,128)}), f32[16,8,128]{2,1,0:T(8,128)S(1)}, u32[]{:S(2)}, u32[]{:S(2)}) async-start(f32[16,8,128]{2,1,0:T(8,128)} %get-tuple-element.34), calls=%async_computation.3 | async-start | bytes 131072 | tf_op jit(solution)/shard_map/all_to_all | solution.py:545
  68.1 3.7 %last.1 = (f32[4,4,384]{2,1,0:T(4,128)S(1)}, f32[4,4,384]{2,1,0:T(4,128)S(1)}, f32[4,4,384]{2,1,0:T(4,128)S(1)}, f32[4,4,384]{2,1,0:T(4,128)S(1)}, f32[4,4,384]{2,1,0:T(4,128)S(1)}) custom-call(s32[2]{0:T(128)S(1)} %pad_add_fusion.meta, s32[32]{0:T(128)S(1)} %get-tuple-element.22.tab, s32[66]{0:T(128)S(1)} %get-tuple-element.28.lst, ...), custom_call_target="tpu_custom_call" | custom-call | flops 200000000 | bytes 8000000 | tf_op jit(solution)/shard_map/last/pallas_call | solution.py:547
  71.8 3.2 %all-to-all-done.3.got = f32[16,8,128]{2,1,0:T(8,128)S(1)} async-done(((f32[16,8,128]{2,1,0:T(8,128)}), f32[16,8,128]{2,1,0:T(8,128)S(1)}, u32[]{:S(2)}, u32[]{:S(2)}) %all-to-all-start.3) | async-done | bytes 65568 | tf_op jit(solution)/shard_map/all_to_all | solution.py:545
  75.0 0.8 %finish.1 = (f32[4,4,384]{2,1,0:T(4,128)}, f32[4,4,384]{2,1,0:T(4,128)}) custom-call(f32[8,128]{1,0:T(8,128)S(1)} %get-tuple-element.33.steps, f32[16,8,128]{2,1,0:T(8,128)S(1)} %all-to-all-done.3.got, f32[4,4,384]{2,1,0:T(4,128)S(1)} %get-tuple-element.37.o_p, f32[4,4,384]{2,1,0:T(4,128)S(1)} %get-tuple-element.38.o_z, ...), custom_call_target="tpu_custom_call" | custom-call | tf_op jit(solution)/shard_map/finish/pallas_call | solution.py:557
  (2 shorter events, 0.0 us)
Async XLA Ops:
  0.6 0.7 copy-start.8
  1.3 0.7 copy-start.9
  2.0 0.7 copy-start
  2.0 0.7 copy-start.2
  2.0 0.7 copy-start.3
  2.0 0.7 copy-start.4
  2.0 0.7 copy-start.5
  2.0 0.7 copy-start.6
  2.1 0.7 copy-start.1
  2.1 0.7 copy-start.7
  5.5 20.1 %all-to-all-start = ((f32[32,24,128]{2,1,0:T(8,128)}), f32[32,24,128]{2,1,0:T(8,128)S(1)}, u32[]{:S(2)}, u32[]{:S(2)}) async-start(f32[32,24,128]{2,1,0:T(8,128)} %bitcast.4), calls=%async_computation | async-start | bytes 786432 | tf_op jit(solution)/shard_map/all_to_all | solution.py:513
  12.9 5.4 %collective-permute-start = (f32[4,16,128]{2,1,0:T(8,128)S(1)}, f32[4,16,128]{2,1,0:T(8,128)S(1)}, u32[]{:S(2)}, u32[]{:S(2)}) collective-permute-start(f32[4,16,128]{2,1,0:T(8,128)S(1)} %get-tuple-element.23), channel_id=1, source_target_pairs={{0,1},{1,0},{2,3},{3,2},{4,5},{5,4},{6,7},{7,6},{8,9},{9,8},{10,11... | collective-permute-start | bytes 98312 | tf_op jit(solution)/shard_map/ppermute | solution.py:508
  64.6 10.4 %all-to-all-start.3 = ((f32[16,8,128]{2,1,0:T(8,128)}), f32[16,8,128]{2,1,0:T(8,128)S(1)}, u32[]{:S(2)}, u32[]{:S(2)}) async-start(f32[16,8,128]{2,1,0:T(8,128)} %get-tuple-element.34), calls=%async_computation.3 | async-start | bytes 131072 | tf_op jit(solution)/shard_map/all_to_all | solution.py:545

commit v2 on v1

--- a/solution.py
+++ b/solution.py
@@ -13,6 +13,7 @@
 HIGH = 4
 CAP = 2
 SUB = 8
+UNROLL = 4
 F32 = jnp.float32
 BF16 = jnp.bfloat16
 
@@ -47,16 +48,22 @@
     return jnp.concatenate([high, low], axis=1)
 
 
-def spread(knot, kinds):
-    low = jnp.bitwise_and(knot, LANES - 1)
+def places():
+    return iota((LANES, LANES), 0).astype(F32).astype(BF16)
+
+
+def spread(place, knot, kinds):
+    low = jnp.bitwise_and(knot, LANES - 1).astype(F32)
     high = jnp.right_shift(knot, 7)
-    hot = jnp.where(iota((LANES, LANES), 0) == jnp.broadcast_to(low[0:1], (LANES, LANES)), 1.0, 0.0)
-    hot = hot.astype(BF16)
+    low = jnp.concatenate([low, low], axis=0).astype(BF16)
+    low = jnp.concatenate([low] * (LANES // 16), axis=0)
+    hot = jnp.where(place == low, jnp.ones((), BF16), jnp.zeros((), BF16))
     hot = jnp.concatenate([hot, hot], axis=1)
-    high32 = jnp.broadcast_to(high[0:1], (4 * SUB, LANES))
     masks = []
     for h in range(HIGH):
-        mask = jnp.where(high32 == h, 1.0, 0.0).astype(BF16)
+        mask = jnp.where(high == h, 1.0, 0.0)
+        mask = jnp.concatenate([mask, mask], axis=0).astype(BF16)
+        mask = jnp.concatenate([mask, mask], axis=0)
         masks.append(jnp.concatenate([mask, mask], axis=1))
     rows = []
     for kind in kinds:
@@ -104,10 +111,12 @@
 
 
 def inc_tile(inc_ref, block, rank):
-    normals = inc_ref[block, pl.ds(pl.multiple_of(rank * SUB, SUB), SUB), :]
-    info = inc_ref[block, 2 * SUB : 3 * SUB, :]
-    info = jnp.where(rank == 0, info, jnp.concatenate([info[4:8], info[0:4]], axis=0))
-    return normals, row_of(info, 0).astype(jnp.int32), basis_of(row_of(info, 1)), row_of(info, 2)
+    tile = jnp.concatenate([inc_ref[block, 2 * rank], inc_ref[block, 2 * rank + 1]], axis=0)
+    info = inc_ref[block, 4]
+    knot = jnp.where(rank == 0, info[0:1], info[1:2])
+    normals = jnp.where(iota((SUB, LANES), 0) < DOF, tile, 0.0)
+    knot = jnp.broadcast_to(knot, (SUB, LANES)).astype(jnp.int32)
+    return normals, knot, basis_of(row_of(tile, 6)), row_of(tile, 7)
 
 
 def decode(code, street_size):
@@ -122,7 +131,7 @@
 
 def send_kernel(
     meta, counts, dev, picks, knot_own, knot_par, match, spline, geometry, weight, resid,
-    send, own, tab, filled, taken, normals_s, info_s, match_s,
+    send, own, tab, filled, taken, normals_s, knots_s, match_s,
 ):
     drives = counts.shape[0]
     lanes = send.shape[0]
@@ -136,7 +145,7 @@
     for a in range(drives):
         for m in range(MATCH):
             e = a * MATCH + m
-            dest = dev[lane * drives + a, m]
+            dest = dev[m, lane * drives + a]
             rank = taken[dest]
             taken[dest] = rank + 1
             tab[e] = dest
@@ -155,12 +164,13 @@
             [knot_own[a : a + 1, :].astype(F32), spline[0, a : a + 1, :], rho] + [zero1] * 5, axis=0
         )
         normals_s[a] = jnp.concatenate(
-            [-(geometry[DOF + d, a : a + 1, :] * root) for d in range(DOF)] + [zero1] * 2, axis=0
+            [-(geometry[DOF + d, a : a + 1, :] * root) for d in range(DOF)]
+            + [spline[1, a : a + 1, :], rho],
+            axis=0,
         )
-        half = [knot_par[a : a + 1, :].astype(F32), spline[1, a : a + 1, :], rho, zero1]
-        info_s[a] = jnp.concatenate(half + half, axis=0)
+        knots_s[a] = jnp.broadcast_to(knot_par[a : a + 1, :].astype(F32), (4, LANES))
         match_s[a] = jnp.broadcast_to(match[a : a + 1, :], (SUB, LANES))
-    row = iota((SUB, LANES), 0)
+    row = iota((4, LANES), 0)
     for j in range(lanes):
         normals = []
         infos = []
@@ -170,17 +180,18 @@
             safe = jnp.maximum(e, 0)
             a = jnp.right_shift(safe, 2)
             m = jnp.where(e < 0, -1, jnp.bitwise_and(safe, 3))
-            pick = picks[lane * drives + a, jnp.bitwise_and(safe, 3)]
+            pick = picks[jnp.bitwise_and(safe, 3), lane * drives + a]
             there = jnp.logical_and(e >= 0, counts[a] > street * LANES)
             flags.append(jnp.where(there, pick + 1, 0).astype(F32))
             normals.append(jnp.where(match_s[a] == m, normals_s[a], 0.0))
-            infos.append(info_s[a])
-        info = jnp.where(row < 4, infos[0], infos[1])
-        info = jnp.where(row == 3, flags[0], jnp.where(row == 7, flags[1], info))
+            infos.append(knots_s[a])
+        info = jnp.where(row == 0, infos[0], infos[1])
+        info = jnp.where(row == 2, flags[0], jnp.where(row == 3, flags[1], info))
         for t in range(street_size):
-            send[j, t, 0:SUB, :] = normals[0]
-            send[j, t, SUB : 2 * SUB, :] = normals[1]
-            send[j, t, 2 * SUB : 3 * SUB, :] = info
+            for r in range(CAP):
+                send[j, t, 2 * r] = normals[r][0:4]
+                send[j, t, 2 * r + 1] = normals[r][4:8]
+            send[j, t, 4] = info
 
 
 def put_values(out_ref, tab, own_ref, inc_ref, lst, tiles_ref):
@@ -193,51 +204,55 @@
             value = gather_value(tiles, knot, basis, normals)
             for m in range(MATCH):
                 e = a * MATCH + m
-                out_ref[tab[e], pl.ds(tab[entries + e] * street_size + s, 1), :] = value
+                out_ref[tab[e], tab[entries + e] * street_size + s] = value
 
     def one(code):
         pick, rank, block, lane, part = decode(code, street_size)
         normals, knot, basis, _ = inc_tile(inc_ref, block, rank)
         value = gather_value([tiles_ref[pick, h] for h in range(HIGH)], knot, basis, normals)
-        out_ref[lane, pl.ds((CAP + rank) * street_size + part, 1), :] = value
+        out_ref[lane, (CAP + rank) * street_size + part] = value
 
     count = lst[lst.shape[0] - 1]
 
-    def two(i, carry):
-        one(lst[2 * i])
-        one(lst[2 * i + 1])
+    def some(i, carry):
+        for j in range(UNROLL):
+            one(lst[UNROLL * i + j])
         return carry
 
-    lax.fori_loop(0, jnp.right_shift(count + 1, 1), two, 0)
+    lax.fori_loop(0, lax.div(count + UNROLL - 1, UNROLL), some, 0)
 
 
 def own_sum(sent, got, tab, a, s, street_size, entries):
     e = a * MATCH
-    total = sent[tab[e], pl.ds(tab[entries + e] * street_size + s, 1), :]
+    total = sent[tab[e], tab[entries + e] * street_size + s]
     for m in range(MATCH):
         e = a * MATCH + m
-        total = total + got[tab[e], pl.ds((CAP + tab[entries + e]) * street_size + s, 1), :]
+        total = total + got[tab[e], (CAP + tab[entries + e]) * street_size + s]
     return total
 
 
 def inc_sum(sent, got, rank, lane, part, street_size):
     return (
-        got[lane, pl.ds(rank * street_size + part, 1), :]
-        + sent[lane, pl.ds((CAP + rank) * street_size + part, 1), :]
-    )
-
-
-def spread_all(acc, own_ref, inc_ref, lst, kinds_own, kinds_inc):
+        got[lane, rank * street_size + part]
+        + sent[lane, (CAP + rank) * street_size + part]
+    )
+
+
+def spread_own(acc, own_ref, kinds_own):
     street_size, drives = own_ref.shape[0], own_ref.shape[1]
+    place = places()
     for a in range(drives):
         total = None
         for s in range(street_size):
             normals, knot, basis, rho = own_tile(own_ref, s, a)
             coeffs = [basis[k] * normals for k in range(4)]
-            part = spread(knot, kinds_own(coeffs, rho, a, s))
+            part = spread(place, knot, kinds_own(coeffs, rho, a, s))
             total = part if total is None else total + part
         acc[a] = total
 
+
+def spread_inc(acc, street_size, inc_ref, lst, kinds_inc):
+    place = places()
     count = lst[lst.shape[0] - 1]
 
     def one(index):
@@ -245,35 +260,42 @@
         normals, knot, basis, rho = inc_tile(inc_ref, block, rank)
         normals = jnp.where(index < count, normals, 0.0)
         coeffs = [basis[k] * normals for k in range(4)]
-        return pick, spread(knot, kinds_inc(coeffs, rho, rank, lane, part))
-
-    def two(i, carry):
-        first = one(2 * i)
-        second = one(2 * i + 1)
-        for pick, value in (first, second):
+        return pick, spread(place, knot, kinds_inc(coeffs, rho, rank, lane, part))
+
+    def some(i, carry):
+        for pick, value in [one(UNROLL * i + j) for j in range(UNROLL)]:
             acc[pick] = acc[pick] + value
         return carry
 
-    lax.fori_loop(0, jnp.right_shift(count + 1, 1), two, 0)
-
-
-def start_kernel(tab, own, inc, grad, diag, direction, out, lst, acc):
+    lax.fori_loop(0, lax.div(count + UNROLL - 1, UNROLL), some, 0)
+
+
+def start_kinds(coeffs, rho, *_):
+    return [[c * rho for c in coeffs], [c * c for c in coeffs]]
+
+
+def own_kernel(own, acc):
+    spread_own(acc, own, start_kinds)
+
+
+def start_kernel(tab, own, inc, begun, grad, diag, direction, out, lst, acc):
     drives = own.shape[1]
+    street_size = own.shape[0]
     blocks = inc.shape[0]
     count = 0
     for b in range(blocks):
-        flags = inc[b, 2 * SUB : 3 * SUB, :].astype(jnp.int32)
+        flags = inc[b, 4].astype(jnp.int32)
         for r in range(CAP):
-            flag = flags[4 * r + 3, 0]
+            flag = flags[2 + r, 0]
             lst[count] = (b * CAP + r) * 4 + flag - 1
             count = count + jnp.where(flag > 0, 1, 0)
-    lst[count] = lst[jnp.maximum(count - 1, 0)]
+    last = lst[jnp.maximum(count - 1, 0)]
+    for i in range(UNROLL - 1):
+        lst[count + i] = last
     lst[lst.shape[0] - 1] = count
 
-    def kinds(coeffs, rho, *_):
-        return [[c * rho for c in coeffs], [c * c for c in coeffs]]
-
-    spread_all(acc, own, inc, lst, kinds, kinds)
+    acc[...] = begun[...]
+    spread_inc(acc, street_size, inc, lst, start_kinds)
     for a in range(drives):
         sums = acc[a]
         gradient = fold_shifts(sums, 0)
@@ -318,7 +340,8 @@
         value = jnp.broadcast_to(value, (SUB, LANES))
         return [[c * value for c in coeffs]]
 
-    spread_all(acc, own, inc, lst, kinds_own, kinds_inc)
+    spread_own(acc, own, kinds_own)
+    spread_inc(acc, street_size, inc, lst, kinds_inc)
     first = jnp.zeros((SUB, LANES), F32)
     second = jnp.zeros((SUB, LANES), F32)
     for a in range(drives):
@@ -335,7 +358,7 @@
     row = scalar_row([first, second])
     rows = 2 * CAP * street_size
     for j in range(out.shape[0]):
-        out[j, rows : rows + 1, :] = row
+        out[j, rows] = row
 
 
 def dots_kernel(tab, grad, diag, direction, image, values, sent, got, resid, precond, steps, out):
@@ -343,9 +366,9 @@
     street_size = values.shape[0] // drives
     entries = drives * MATCH
     rows = 2 * CAP * street_size
-    total = got[0, rows : rows + 1, :]
+    total = got[0, rows]
     for j in range(1, got.shape[0]):
-        total = total + got[j, rows : rows + 1, :]
+        total = total + got[j, rows]
     inner = pick_lane(total, 0)
     curve = pick_lane(total, 1)
     alpha = inner / curve
@@ -401,7 +424,8 @@
         value = jnp.broadcast_to(value, (SUB, LANES))
         return [[c * value for c in coeffs]]
 
-    spread_all(acc, own, inc, lst, kinds_own, kinds_inc)
+    spread_own(acc, own, kinds_own)
+    spread_inc(acc, street_size, inc, lst, kinds_inc)
     for a in range(drives):
         sums = fold_shifts(acc[a], 0)
         for h in range(HIGH):
@@ -486,7 +510,7 @@
     send, mine, tab = call(
         send_kernel,
         [
-            ((lanes, street_size, 3 * SUB, LANES), F32),
+            ((lanes, street_size, 5, 4, LANES), F32),
             ((drives, 2 * SUB, LANES), F32),
             ((2 * entries,), jnp.int32),
         ],
@@ -496,12 +520,12 @@
             pltpu.SMEM((CAP * lanes,), jnp.int32),
             pltpu.SMEM((lanes,), jnp.int32),
             pltpu.VMEM((drives, SUB, LANES), F32),
-            pltpu.VMEM((drives, SUB, LANES), F32),
+            pltpu.VMEM((drives, 4, LANES), F32),
             pltpu.VMEM((drives, SUB, LANES), jnp.int32),
         ],
         name="send",
     )(
-        meta, pt_count, partner_dev, partner_pick, knot_own, knot_partner, match_slot,
+        meta, pt_count, partner_dev.T, partner_pick.T, knot_own, knot_partner, match_slot,
         spline, geometry, point_weight, point_resid,
     )
     if street_size == 2:
@@ -511,20 +535,28 @@
     else:
         own = lax.all_gather(mine, "street", axis=0, tiled=False)
     inc = lax.all_to_all(
-        send.reshape(blocks, 3 * SUB, LANES), ("drive", "street"), split_axis=0, concat_axis=0, tiled=True
-    )
-    exchange = ((lanes, 2 * CAP * street_size, LANES), F32)
-    exchange2 = ((lanes, 2 * CAP * street_size + SUB, LANES), F32)
+        send.reshape(blocks, 5, 4, LANES), ("drive", "street"), split_axis=0, concat_axis=0, tiled=True
+    )
+    exchange = ((lanes, 2 * CAP * street_size, 1, LANES), F32)
+    exchange2 = ((lanes, 2 * CAP * street_size + 1, 1, LANES), F32)
     acc = pltpu.VMEM((drives, 128, LANES), F32)
-    list_size = CAP * blocks + 2
+    list_size = CAP * blocks + UNROLL
+    (begun,) = call(
+        own_kernel,
+        [((drives, 256, LANES), F32)],
+        "v",
+        "v",
+        name="own",
+        cost_estimate=pl.CostEstimate(flops=70000000, bytes_accessed=1000000, transcendentals=0),
+    )(own)
     grad, diag, direction, sent, lst = call(
         start_kernel,
         [param, param, param, exchange, ((list_size,), jnp.int32)],
-        "svv",
+        "svvv",
         "vvvvs",
         [pltpu.VMEM((drives, 256, LANES), F32)],
         name="start",
-    )(tab, own, inc)
+    )(tab, own, inc, begun)
     got = lax.all_to_all(sent, "drive", split_axis=0, concat_axis=0, tiled=True)
     image, values, sent2 = call(
         middle_kernel,

time: 76.7 us -> 67.4 us (0.88); the launches traced: 75.8 us -> 67.3 us
  Pallas kernels: 19.1 us -> 14.7 us
  blocking collectives: 27.1 us -> 24.3 us
    all_to_all x1, blocking collectives: 13.4 us -> 11.4 us  [body(): lax.all_to_all(sent2, 'drive', split_axis=0, concat_axis=0, tiled=True)]
    pallas_call x1, Pallas kernels: 5.82 us -> 4.15 us  [body(): call(start_kernel, [param, param, param, exchange, ((list_size,), jnp.int...]
    pallas_call x1, Pallas kernels: 4.69 us -> 3.35 us  [body(): call(middle_kernel, [param, ((street_size * drives, LANES), F32), exchang...]
    all_to_all x1, waiting for transfers between devices: 7.32 us -> 6.1 us  [body(): lax.all_to_all(send.reshape(blocks, 5, 4, LANES), ('drive', 'street'), sp...]
    pallas_call x1, Pallas kernels: 3.68 us -> 2.83 us  [body(): call(last_kernel, [shape] * 5, 'sssvvvvvvvvvvvv', 'vvvvv', [acc, pltpu.VM...]
    all_to_all x1, waiting for transfers between devices: 3.18 us -> 4.02 us  [body(): lax.all_to_all(sent3, 'drive', split_axis=0, concat_axis=0, tiled=True)]
    all_to_all x1, blocking collectives: 13.8 us -> 12.9 us  [body(): got = lax.all_to_all(sent, 'drive', split_axis=0, concat_axis=0, tiled=True)]
    unnamed x22 -> x20, local copies, waits for them, and re-layouts: 2.07 us -> 1.43 us
where the time goes in v2:
time: 67.4 us; the launch traced here: 67.3 us
  blocking collectives  24.3 us (36%)
  Pallas kernels  14.7 us (22%)
  waiting for transfers between devices  13.4 us (20%)
  starting transfers between devices  12.6 us (19%)
  local copies, waits for them, and re-layouts  1.43 us (2%)
  between operations  0.76 us (1%)
    all_to_all x1, blocking collectives, body(): got = lax.all_to_all(sent, 'drive', split_axis=0, concat_axis=0, tiled=True)  12.9 us
    all_to_all x1, blocking collectives, body(): lax.all_to_all(sent2, 'drive', split_axis=0, concat_axis=0, tiled=True)  11.4 us
    all_to_all x1, starting transfers between devices, body(): lax.all_to_all(send.reshape(blocks, 5, 4, LANES), ('drive', 'street'), sp...  7.3 us
    all_to_all x1, waiting for transfers between devices, body(): lax.all_to_all(send.reshape(blocks, 5, 4, LANES), ('drive', 'street'), sp...  6.1 us
    pallas_call x1, Pallas kernels, body(): call(start_kernel, [param, param, param, exchange, ((list_size,), jnp.int...  4.15 us
    all_to_all x1, waiting for transfers between devices, body(): lax.all_to_all(sent3, 'drive', split_axis=0, concat_axis=0, tiled=True)  4.02 us
    all_to_all x1, starting transfers between devices, body(): lax.all_to_all(sent3, 'drive', split_axis=0, concat_axis=0, tiled=True)  3.49 us
    pallas_call x1, Pallas kernels, body(): call(middle_kernel, [param, ((street_size * drives, LANES), F32), exchang...  3.35 us
  transfers between devices with their start and end apart: 3, of which 3 were waited for; matrix products, arithmetic and copies ran while one was open for 0% of the time, Pallas kernels for 5%

profile of v2, /device:TPU:0, one launch (start us, length us, event | category | flops | bytes accessed | tf_op | source)
XLA Modules:
  0.0 67.3 jit_solution(13345687059905930491)
XLA Ops:
  0.6 0.0 copy-start.8
  0.6 0.0 copy-start.7
  0.7 0.0 copy-start.6
  0.7 0.0 copy-start.5
  0.7 0.0 copy-start.4
  0.7 0.0 copy-start.3
  0.7 0.0 copy-start.1
  0.7 0.1 pad_add_fusion.meta
  0.8 0.0 copy-start.2
  0.8 0.0 copy-start.9
  0.8 0.5 copy-done.8
  1.3 0.0 copy-done.7
  1.3 0.0 copy-done.6
  1.4 0.0 copy-done.5
  1.4 0.0 copy-done.4
  1.4 0.0 copy-done.3
  1.4 0.0 copy-done.1
  1.4 0.0 copy-done.2
  1.5 0.0 copy-done.9
  1.5 0.0 copy-start
  1.5 0.7 %copy-done = f32[12,4,128]{2,1,0:T(4,128)S(1)} copy-done((f32[12,4,128]{2,1,0:T(4,128)S(1)}, f32[12,4,128]{2,1,0:T(4,128)}, u32[]{:S(2)}) %copy-start) | copy-done | bytes 24600
  2.2 1.7 %send.1 = (f32[16,2,5,4,128]{4,3,2,1,0:T(4,128)}, f32[4,16,128]{2,1,0:T(8,128)S(1)}, s32[32]{0:T(128)S(1)}) custom-call(s32[2]{0:T(128)S(1)} %pad_add_fusion.meta, s32[4]{0:T(128)S(1)} %copy-done.9, s32[4,64]{1,0:T(4,128)S(1)} %bitcast.9, s32[4,64]{1,0:T(4,128)S(1)} %bitcast.10, s32[4,128]{1,0:T(4,128)S(1)} %copy-done.4, s32[4,128]{1,0:T(4,128)S(1)} %copy-done.5, ...), custom_call_target="tpu_custom_call" | custom-call | tf_op jit(solution)/shard_map/send/pallas_call | solution.py:510
  3.9 7.3 %all-to-all-start = ((f32[32,5,4,128]{3,2,1,0:T(4,128)}), f32[32,5,4,128]{3,2,1,0:T(4,128)S(1)}, u32[]{:S(2)}, u32[]{:S(2)}) async-start(f32[32,5,4,128]{3,2,1,0:T(4,128)} %bitcast.6), calls=%async_computation | async-start | bytes 655360 | tf_op jit(solution)/shard_map/all_to_all | solution.py:537
  11.2 1.8 %collective-permute-start = (f32[4,16,128]{2,1,0:T(8,128)S(1)}, f32[4,16,128]{2,1,0:T(8,128)S(1)}, u32[]{:S(2)}, u32[]{:S(2)}) collective-permute-start(f32[4,16,128]{2,1,0:T(8,128)S(1)} %get-tuple-element.23), channel_id=1, source_target_pairs={{0,1},{1,0},{2,3},{3,2},{4,5},{5,4},{6,7},{7,6},{8,9},{9,8},{10,11... | collective-permute-start | bytes 98312 | tf_op jit(solution)/shard_map/ppermute | solution.py:532
  13.1 3.3 %collective-permute-done = f32[4,16,128]{2,1,0:T(8,128)S(1)} collective-permute-done((f32[4,16,128]{2,1,0:T(8,128)S(1)}, f32[4,16,128]{2,1,0:T(8,128)S(1)}, u32[]{:S(2)}, u32[]{:S(2)}) %collective-permute-start) | collective-permute-done | bytes 32800 | tf_op jit(solution)/shard_map/ppermute | solution.py:532
  16.4 0.4 own.1.begun
  16.8 6.1 %all-to-all-done.inc = f32[32,5,4,128]{3,2,1,0:T(4,128)S(1)} async-done(((f32[32,5,4,128]{3,2,1,0:T(4,128)}), f32[32,5,4,128]{3,2,1,0:T(4,128)S(1)}, u32[]{:S(2)}, u32[]{:S(2)}) %all-to-all-start) | async-done | bytes 327712 | tf_op jit(solution)/shard_map/all_to_all | solution.py:537
  22.9 4.1 %start.1 = (f32[4,4,8,128]{3,2,1,0:T(8,128)S(1)}, f32[4,4,8,128]{3,2,1,0:T(8,128)S(1)}, f32[4,4,8,128]{3,2,1,0:T(8,128)S(1)}, f32[16,8,1,128]{3,2,1,0:T(1,128)S(1)}, s32[68]{0:T(128)S(1)}) custom-call(s32[32]{0:T(128)S(1)} %get-tuple-element.22.tab, f32[2,4,16,128]{3,2,1,0:T(8,128)S(1)} %pad_maximum_fusion.own, f32[32,5,4,128]{3,2,1,0:T(4,128)S(1)} %all-to-all-done.inc, ...), custom_call_target="tpu_custom_call" | custom-call | tf_op jit(solution)/shard_map/start/pallas_call | solution.py:552
  27.1 12.9 %all_to_all.20.got = f32[16,8,1,128]{3,2,1,0:T(1,128)S(1)} all-to-all(f32[16,8,1,128]{3,2,1,0:T(1,128)S(1)} %get-tuple-element.29.sent), channel_id=1, replica_groups=mesh['region'=1,'drive'=16,'street'=2] {'drive'}, dimensions={0} | all-to-all | bytes 131072 | tf_op jit(solution)/shard_map/all_to_all | solution.py:560
  40.0 3.4 %middle.1 = (f32[4,4,8,128]{3,2,1,0:T(8,128)S(1)}, f32[8,128]{1,0:T(8,128)S(1)}, f32[16,9,1,128]{3,2,1,0:T(1,128)S(1)}) custom-call(s32[32]{0:T(128)S(1)} %get-tuple-element.22.tab, s32[68]{0:T(128)S(1)} %get-tuple-element.28.lst, f32[2,4,16,128]{3,2,1,0:T(8,128)S(1)} %pad_maximum_fusion.own, f32[32,5,4,128]{3,2,1,0:T(4,128)S(1)} %all-to-all-done.inc, ...), custom_call_target="tpu_custom_call" | custom-call | tf_op jit(solution)/shard_map/middle/pallas_call | solution.py:561
  43.4 11.4 %all_to_all.21.got.got2 = f32[16,9,1,128]{3,2,1,0:T(1,128)S(1)} all-to-all(f32[16,9,1,128]{3,2,1,0:T(1,128)S(1)} %get-tuple-element.32.sent.sent2), channel_id=1, replica_groups=mesh['region'=1,'drive'=16,'street'=2] {'drive'}, dimensions={0} | all-to-all | bytes 147456 | tf_op jit(solution)/shard_map/all_to_all | solution.py:569
  54.8 1.4 %dots.1 = (f32[4,4,8,128]{3,2,1,0:T(8,128)S(1)}, f32[4,4,8,128]{3,2,1,0:T(8,128)S(1)}, f32[8,128]{1,0:T(8,128)S(1)}, f32[16,8,128]{2,1,0:T(8,128)}) custom-call(s32[32]{0:T(128)S(1)} %get-tuple-element.22.tab, f32[4,4,8,128]{3,2,1,0:T(8,128)S(1)} %get-tuple-element.25.grad, f32[4,4,8,128]{3,2,1,0:T(8,128)S(1)} %get-tuple-element.26.diag, ...), custom_call_target="tpu_custom_call" | custom-call | tf_op jit(solution)/shard_map/dots/pallas_call | solution.py:570
  56.1 3.5 %all-to-all-start.3 = ((f32[16,8,128]{2,1,0:T(8,128)}), f32[16,8,128]{2,1,0:T(8,128)S(1)}, u32[]{:S(2)}, u32[]{:S(2)}) async-start(f32[16,8,128]{2,1,0:T(8,128)} %get-tuple-element.34), calls=%async_computation.3 | async-start | bytes 131072 | tf_op jit(solution)/shard_map/all_to_all | solution.py:577
  59.6 2.8 %last.1 = (f32[4,4,384]{2,1,0:T(4,128)S(1)}, f32[4,4,384]{2,1,0:T(4,128)S(1)}, f32[4,4,384]{2,1,0:T(4,128)S(1)}, f32[4,4,384]{2,1,0:T(4,128)S(1)}, f32[4,4,384]{2,1,0:T(4,128)S(1)}) custom-call(s32[2]{0:T(128)S(1)} %pad_add_fusion.meta, s32[32]{0:T(128)S(1)} %get-tuple-element.22.tab, s32[68]{0:T(128)S(1)} %get-tuple-element.28.lst, ...), custom_call_target="tpu_custom_call" | custom-call | flops 200000000 | bytes 8000000 | tf_op jit(solution)/shard_map/last/pallas_call | solution.py:579
  62.5 4.0 %all-to-all-done.3.got = f32[16,8,128]{2,1,0:T(8,128)S(1)} async-done(((f32[16,8,128]{2,1,0:T(8,128)}), f32[16,8,128]{2,1,0:T(8,128)S(1)}, u32[]{:S(2)}, u32[]{:S(2)}) %all-to-all-start.3) | async-done | bytes 65568 | tf_op jit(solution)/shard_map/all_to_all | solution.py:577
  66.5 0.8 %finish.1 = (f32[4,4,384]{2,1,0:T(4,128)}, f32[4,4,384]{2,1,0:T(4,128)}) custom-call(f32[8,128]{1,0:T(8,128)S(1)} %get-tuple-element.33.steps, f32[16,8,128]{2,1,0:T(8,128)S(1)} %all-to-all-done.3.got, f32[4,4,384]{2,1,0:T(4,128)S(1)} %get-tuple-element.37.o_p, f32[4,4,384]{2,1,0:T(4,128)S(1)} %get-tuple-element.38.o_z, ...), custom_call_target="tpu_custom_call" | custom-call | tf_op jit(solution)/shard_map/finish/pallas_call | solution.py:589
  (2 shorter events, 0.0 us)
Async XLA Ops:
  0.6 0.7 %copy-start.8 = (f32[4,128]{1,0:T(4,128)S(1)}, f32[4,128]{1,0:T(4,128)}, u32[]{:S(2)}) copy-start(f32[4,128]{1,0:T(4,128)} %resid.1) | copy-start | bytes 6148
  0.6 0.7 %copy-start.7 = (f32[4,128]{1,0:T(4,128)S(1)}, f32[4,128]{1,0:T(4,128)}, u32[]{:S(2)}) copy-start(f32[4,128]{1,0:T(4,128)} %weight.1) | copy-start | bytes 6148
  0.7 0.7 %copy-start.6 = (s32[4,128]{1,0:T(4,128)S(1)}, s32[4,128]{1,0:T(4,128)}, u32[]{:S(2)}) copy-start(s32[4,128]{1,0:T(4,128)} %match.1) | copy-start | bytes 6148
  0.7 0.7 %copy-start.5 = (s32[4,128]{1,0:T(4,128)S(1)}, s32[4,128]{1,0:T(4,128)}, u32[]{:S(2)}) copy-start(s32[4,128]{1,0:T(4,128)} %knot_par.1) | copy-start | bytes 6148
  0.7 0.7 %copy-start.4 = (s32[4,128]{1,0:T(4,128)S(1)}, s32[4,128]{1,0:T(4,128)}, u32[]{:S(2)}) copy-start(s32[4,128]{1,0:T(4,128)} %knot_own.1) | copy-start | bytes 6148
  0.7 0.7 %copy-start.3 = (s32[64,4]{0,1:T(4,128)S(1)}, s32[64,4]{0,1:T(4,128)}, u32[]{:S(2)}) copy-start(s32[64,4]{0,1:T(4,128)} %param.12) | copy-start | bytes 3076
  0.7 0.7 %copy-start.1 = (f32[2,4,128]{2,1,0:T(4,128)S(1)}, f32[2,4,128]{2,1,0:T(4,128)}, u32[]{:S(2)}) copy-start(f32[2,4,128]{2,1,0:T(4,128)} %spline.1) | copy-start | bytes 12292
  0.8 0.7 %copy-start.2 = (s32[64,4]{0,1:T(4,128)S(1)}, s32[64,4]{0,1:T(4,128)}, u32[]{:S(2)}) copy-start(s32[64,4]{0,1:T(4,128)} %param.11) | copy-start | bytes 3076
  0.8 0.7 %copy-start.9 = (s32[4]{0:T(128)S(1)}, s32[4]{0:T(128)}, u32[]{:S(2)}) copy-start(s32[4]{0:T(128)} %counts.1) | copy-start | bytes 52
  1.5 0.7 %copy-start = (f32[12,4,128]{2,1,0:T(4,128)S(1)}, f32[12,4,128]{2,1,0:T(4,128)}, u32[]{:S(2)}) copy-start(f32[12,4,128]{2,1,0:T(4,128)} %geometry.1) | copy-start | bytes 73732
  3.9 19.0 %all-to-all-start = ((f32[32,5,4,128]{3,2,1,0:T(4,128)}), f32[32,5,4,128]{3,2,1,0:T(4,128)S(1)}, u32[]{:S(2)}, u32[]{:S(2)}) async-start(f32[32,5,4,128]{3,2,1,0:T(4,128)} %bitcast.6), calls=%async_computation | async-start | bytes 655360 | tf_op jit(solution)/shard_map/all_to_all | solution.py:537
  11.2 5.1 %collective-permute-start = (f32[4,16,128]{2,1,0:T(8,128)S(1)}, f32[4,16,128]{2,1,0:T(8,128)S(1)}, u32[]{:S(2)}, u32[]{:S(2)}) collective-permute-start(f32[4,16,128]{2,1,0:T(8,128)S(1)} %get-tuple-element.23), channel_id=1, source_target_pairs={{0,1},{1,0},{2,3},{3,2},{4,5},{5,4},{6,7},{7,6},{8,9},{9,8},{10,11... | collective-permute-start | bytes 98312 | tf_op jit(solution)/shard_map/ppermute | solution.py:532
  56.1 10.4 %all-to-all-start.3 = ((f32[16,8,128]{2,1,0:T(8,128)}), f32[16,8,128]{2,1,0:T(8,128)S(1)}, u32[]{:S(2)}, u32[]{:S(2)}) async-start(f32[16,8,128]{2,1,0:T(8,128)} %get-tuple-element.34), calls=%async_computation.3 | async-start | bytes 131072 | tf_op jit(solution)/shard_map/all_to_all | solution.py:577

commit v3 on v2

--- a/solution.py
+++ b/solution.py
@@ -13,7 +13,7 @@
 HIGH = 4
 CAP = 2
 SUB = 8
-UNROLL = 4
+UNROLL = 13
 F32 = jnp.float32
 BF16 = jnp.bfloat16
 
@@ -65,13 +65,14 @@
         mask = jnp.concatenate([mask, mask], axis=0).astype(BF16)
         mask = jnp.concatenate([mask, mask], axis=0)
         masks.append(jnp.concatenate([mask, mask], axis=1))
-    rows = []
+    sums = []
     for kind in kinds:
         parts = split_two(jnp.concatenate(kind, axis=0))
-        for h in range(HIGH):
-            rows.append(parts * masks[h])
-    left = jnp.concatenate(rows, axis=0)
-    return lax.dot_general(left, hot, (((1,), (1,)), ((), ())), preferred_element_type=F32)
+        left = jnp.concatenate([parts * mask for mask in masks], axis=0)
+        sums.append(
+            lax.dot_general(left, hot, (((1,), (1,)), ((), ())), preferred_element_type=F32)
+        )
+    return jnp.concatenate(sums, axis=0)
 
 
 def fold_shifts(acc, base):
@@ -124,8 +125,10 @@
     tile = jnp.right_shift(code, 2)
     rank = jnp.bitwise_and(tile, 1)
     block = jnp.right_shift(tile, 1)
-    lane = lax.div(block, street_size)
-    part = block - lane * street_size
+    shift = street_size.bit_length() - 1
+    assert street_size == 1 << shift
+    lane = jnp.right_shift(block, shift)
+    part = jnp.bitwise_and(block, street_size - 1)
     return pick, rank, block, lane, part
 
 
@@ -283,12 +286,16 @@
     street_size = own.shape[0]
     blocks = inc.shape[0]
     count = 0
-    for b in range(blocks):
-        flags = inc[b, 4].astype(jnp.int32)
-        for r in range(CAP):
-            flag = flags[2 + r, 0]
-            lst[count] = (b * CAP + r) * 4 + flag - 1
-            count = count + jnp.where(flag > 0, 1, 0)
+    for first in range(0, blocks, 4):
+        digits = inc[first, 4]
+        for i in range(1, 4):
+            digits = digits + inc[first + i, 4] * float(8**i)
+        digits = (digits[2:3] + digits[3:4] * float(8**4)).astype(jnp.int32)[0, 0]
+        for i in range(4):
+            for r in range(CAP):
+                flag = jnp.bitwise_and(jnp.right_shift(digits, 3 * (4 * r + i)), 7)
+                lst[count] = ((first + i) * CAP + r) * 4 + flag - 1
+                count = count + jnp.where(flag > 0, 1, 0)
     last = lst[jnp.maximum(count - 1, 0)]
     for i in range(UNROLL - 1):
         lst[count + i] = last
@@ -395,7 +402,7 @@
     head = iota((SUB, LANES), 0) == 0
     two = two + jnp.where(head, jnp.broadcast_to(slots2, (SUB, LANES)), 0.0)
     three = three + jnp.where(head, jnp.broadcast_to(slots3, (SUB, LANES)), 0.0)
-    row = jnp.broadcast_to(scalar_row([one, two, three]), (SUB, LANES))
+    row = scalar_row([one, two, three])
     for j in range(out.shape[0]):
         out[j] = row
     lane = iota((SUB, LANES), 1)
@@ -461,7 +468,6 @@
     total = got[0]
     for j in range(1, got.shape[0]):
         total = total + got[j]
-    total = total[0:1, :]
     inner_next = pick_lane(total, 0)
     alpha = steps[0:1, 0:1]
     inner = steps[0:1, 1:2]
@@ -507,6 +513,10 @@
     entries = drives * MATCH
     blocks = lanes * street_size
     param = ((drives, HIGH, SUB, LANES), F32)
+    arrays = (
+        pt_count, partner_dev.T, partner_pick.T, knot_own, knot_partner, match_slot,
+        spline, geometry, point_weight, point_resid,
+    )
     send, mine, tab = call(
         send_kernel,
         [
@@ -524,10 +534,7 @@
             pltpu.VMEM((drives, SUB, LANES), jnp.int32),
         ],
         name="send",
-    )(
-        meta, pt_count, partner_dev.T, partner_pick.T, knot_own, knot_partner, match_slot,
-        spline, geometry, point_weight, point_resid,
-    )
+    )(meta, *arrays)
     if street_size == 2:
         peer = lax.ppermute(mine, "street", [(0, 1), (1, 0)])
         first = meta[1] == 0
@@ -569,7 +576,7 @@
     got2 = lax.all_to_all(sent2, "drive", split_axis=0, concat_axis=0, tiled=True)
     resid, precond, steps, sent3 = call(
         dots_kernel,
-        [param, param, ((SUB, LANES), F32), ((lanes, SUB, LANES), F32)],
+        [param, param, ((SUB, LANES), F32), ((lanes, 1, LANES), F32)],
         "svvvvvvv",
         "vvvv",
         name="dots",

time: 67.4 us -> 62.6 us (0.929)
  blocking collectives: 24.3 us -> 19.6 us
    all_to_all x1, blocking collectives: 12.9 us -> 10 us  [body(): got = lax.all_to_all(sent, 'drive', split_axis=0, concat_axis=0, tiled=True)]
    all_to_all x1, blocking collectives: 11.4 us -> 9.59 us  [body(): lax.all_to_all(sent2, 'drive', split_axis=0, concat_axis=0, tiled=True)]
where the time goes in v3:
time: 62.6 us; the launch traced here: 62 us
  blocking collectives  19.6 us (31%)
  Pallas kernels  14.6 us (23%)
  waiting for transfers between devices  12.9 us (21%)
  starting transfers between devices  12.6 us (20%)
  local copies, waits for them, and re-layouts  1.43 us (2%)
  between operations  0.76 us (1%)
    all_to_all x1, blocking collectives, body(): got = lax.all_to_all(sent, 'drive', split_axis=0, concat_axis=0, tiled=True)  10 us
    all_to_all x1, blocking collectives, body(): lax.all_to_all(sent2, 'drive', split_axis=0, concat_axis=0, tiled=True)  9.59 us
    all_to_all x1, starting transfers between devices, body(): lax.all_to_all(send.reshape(blocks, 5, 4, LANES), ('drive', 'street'), sp...  7.3 us
    all_to_all x1, waiting for transfers between devices, body(): lax.all_to_all(send.reshape(blocks, 5, 4, LANES), ('drive', 'street'), sp...  6.1 us
    pallas_call x1, Pallas kernels, body(): call(start_kernel, [param, param, param, exchange, ((list_size,), jnp.int...  3.99 us
    pallas_call x1, Pallas kernels, body(): call(middle_kernel, [param, ((street_size * drives, LANES), F32), exchang...  3.5 us
    all_to_all x1, starting transfers between devices, body(): lax.all_to_all(sent3, 'drive', split_axis=0, concat_axis=0, tiled=True)  3.47 us
    all_to_all x1, waiting for transfers between devices, body(): lax.all_to_all(sent3, 'drive', split_axis=0, concat_axis=0, tiled=True)  3.46 us
  transfers between devices with their start and end apart: 3, of which 3 were waited for; matrix products, arithmetic and copies ran while one was open for 0% of the time, Pallas kernels for 5%

profile of v3, /device:TPU:0, one launch (start us, length us, event | category | flops | bytes accessed | tf_op | source)
XLA Modules:
  0.0 62.0 jit_solution(4107476932550163622)
XLA Ops:
  0.6 0.0 copy-start.8
  0.6 0.0 copy-start.7
  0.7 0.0 copy-start.6
  0.7 0.0 copy-start.5
  0.7 0.0 copy-start.4
  0.7 0.0 copy-start.3
  0.7 0.0 copy-start.1
  0.7 0.1 pad_add_fusion.meta
  0.8 0.0 copy-start.2
  0.8 0.0 copy-start.9
  0.8 0.5 copy-done.8
  1.3 0.0 copy-done.7
  1.3 0.0 copy-done.6
  1.4 0.0 copy-done.5
  1.4 0.0 copy-done.4
  1.4 0.0 copy-done.3
  1.4 0.0 copy-done.1
  1.4 0.0 copy-done.2
  1.5 0.0 copy-done.9
  1.5 0.0 copy-start
  1.5 0.7 %copy-done = f32[12,4,128]{2,1,0:T(4,128)S(1)} copy-done((f32[12,4,128]{2,1,0:T(4,128)S(1)}, f32[12,4,128]{2,1,0:T(4,128)}, u32[]{:S(2)}) %copy-start) | copy-done | bytes 24600
  2.2 1.7 %send.1 = (f32[16,2,5,4,128]{4,3,2,1,0:T(4,128)}, f32[4,16,128]{2,1,0:T(8,128)S(1)}, s32[32]{0:T(128)S(1)}) custom-call(s32[2]{0:T(128)S(1)} %pad_add_fusion.meta, s32[4]{0:T(128)S(1)} %copy-done.9, s32[4,64]{1,0:T(4,128)S(1)} %bitcast.9, s32[4,64]{1,0:T(4,128)S(1)} %bitcast.10, s32[4,128]{1,0:T(4,128)S(1)} %copy-done.4, s32[4,128]{1,0:T(4,128)S(1)} %copy-done.5, ...), custom_call_target="tpu_custom_call" | custom-call | tf_op jit(solution)/shard_map/send/pallas_call | solution.py:520
  3.9 7.3 %all-to-all-start = ((f32[32,5,4,128]{3,2,1,0:T(4,128)}), f32[32,5,4,128]{3,2,1,0:T(4,128)S(1)}, u32[]{:S(2)}, u32[]{:S(2)}) async-start(f32[32,5,4,128]{3,2,1,0:T(4,128)} %bitcast.6), calls=%async_computation | async-start | bytes 655360 | tf_op jit(solution)/shard_map/all_to_all | solution.py:544
  11.2 1.8 %collective-permute-start = (f32[4,16,128]{2,1,0:T(8,128)S(1)}, f32[4,16,128]{2,1,0:T(8,128)S(1)}, u32[]{:S(2)}, u32[]{:S(2)}) collective-permute-start(f32[4,16,128]{2,1,0:T(8,128)S(1)} %get-tuple-element.23), channel_id=1, source_target_pairs={{0,1},{1,0},{2,3},{3,2},{4,5},{5,4},{6,7},{7,6},{8,9},{9,8},{10,11... | collective-permute-start | bytes 98312 | tf_op jit(solution)/shard_map/ppermute | solution.py:539
  13.1 3.3 %collective-permute-done = f32[4,16,128]{2,1,0:T(8,128)S(1)} collective-permute-done((f32[4,16,128]{2,1,0:T(8,128)S(1)}, f32[4,16,128]{2,1,0:T(8,128)S(1)}, u32[]{:S(2)}, u32[]{:S(2)}) %collective-permute-start) | collective-permute-done | bytes 32800 | tf_op jit(solution)/shard_map/ppermute | solution.py:539
  16.4 0.4 own.1.begun
  16.8 6.1 %all-to-all-done.inc = f32[32,5,4,128]{3,2,1,0:T(4,128)S(1)} async-done(((f32[32,5,4,128]{3,2,1,0:T(4,128)}), f32[32,5,4,128]{3,2,1,0:T(4,128)S(1)}, u32[]{:S(2)}, u32[]{:S(2)}) %all-to-all-start) | async-done | bytes 327712 | tf_op jit(solution)/shard_map/all_to_all | solution.py:544
  22.9 4.0 %start.1 = (f32[4,4,8,128]{3,2,1,0:T(8,128)S(1)}, f32[4,4,8,128]{3,2,1,0:T(8,128)S(1)}, f32[4,4,8,128]{3,2,1,0:T(8,128)S(1)}, f32[16,8,1,128]{3,2,1,0:T(1,128)S(1)}, s32[77]{0:T(128)S(1)}) custom-call(s32[32]{0:T(128)S(1)} %get-tuple-element.22.tab, f32[2,4,16,128]{3,2,1,0:T(8,128)S(1)} %pad_maximum_fusion.own, f32[32,5,4,128]{3,2,1,0:T(4,128)S(1)} %all-to-all-done.inc, ...), custom_call_target="tpu_custom_call" | custom-call | tf_op jit(solution)/shard_map/start/pallas_call | solution.py:559
  26.9 10.0 %all_to_all.20.got = f32[16,8,1,128]{3,2,1,0:T(1,128)S(1)} all-to-all(f32[16,8,1,128]{3,2,1,0:T(1,128)S(1)} %get-tuple-element.29.sent), channel_id=1, replica_groups=mesh['region'=1,'drive'=16,'street'=2] {'drive'}, dimensions={0} | all-to-all | bytes 131072 | tf_op jit(solution)/shard_map/all_to_all | solution.py:567
  37.0 3.5 %middle.1 = (f32[4,4,8,128]{3,2,1,0:T(8,128)S(1)}, f32[8,128]{1,0:T(8,128)S(1)}, f32[16,9,1,128]{3,2,1,0:T(1,128)S(1)}) custom-call(s32[32]{0:T(128)S(1)} %get-tuple-element.22.tab, s32[77]{0:T(128)S(1)} %get-tuple-element.28.lst, f32[2,4,16,128]{3,2,1,0:T(8,128)S(1)} %pad_maximum_fusion.own, f32[32,5,4,128]{3,2,1,0:T(4,128)S(1)} %all-to-all-done.inc, ...), custom_call_target="tpu_custom_call" | custom-call | tf_op jit(solution)/shard_map/middle/pallas_call | solution.py:568
  40.5 9.6 %all_to_all.21.got.got2 = f32[16,9,1,128]{3,2,1,0:T(1,128)S(1)} all-to-all(f32[16,9,1,128]{3,2,1,0:T(1,128)S(1)} %get-tuple-element.32.sent.sent2), channel_id=1, replica_groups=mesh['region'=1,'drive'=16,'street'=2] {'drive'}, dimensions={0} | all-to-all | bytes 147456 | tf_op jit(solution)/shard_map/all_to_all | solution.py:576
  50.0 1.4 %dots.1 = (f32[4,4,8,128]{3,2,1,0:T(8,128)S(1)}, f32[4,4,8,128]{3,2,1,0:T(8,128)S(1)}, f32[8,128]{1,0:T(8,128)S(1)}, f32[16,1,128]{2,1,0:T(1,128)}) custom-call(s32[32]{0:T(128)S(1)} %get-tuple-element.22.tab, f32[4,4,8,128]{3,2,1,0:T(8,128)S(1)} %get-tuple-element.25.grad, f32[4,4,8,128]{3,2,1,0:T(8,128)S(1)} %get-tuple-element.26.diag, ...), custom_call_target="tpu_custom_call" | custom-call | tf_op jit(solution)/shard_map/dots/pallas_call | solution.py:577
  51.4 3.5 %all-to-all-start.3 = ((f32[16,1,128]{2,1,0:T(1,128)}), f32[16,1,128]{2,1,0:T(1,128)S(1)}, u32[]{:S(2)}, u32[]{:S(2)}) async-start(f32[16,1,128]{2,1,0:T(1,128)} %get-tuple-element.34), calls=%async_computation.3 | async-start | bytes 16384 | tf_op jit(solution)/shard_map/all_to_all | solution.py:584
  54.9 2.8 %last.1 = (f32[4,4,384]{2,1,0:T(4,128)S(1)}, f32[4,4,384]{2,1,0:T(4,128)S(1)}, f32[4,4,384]{2,1,0:T(4,128)S(1)}, f32[4,4,384]{2,1,0:T(4,128)S(1)}, f32[4,4,384]{2,1,0:T(4,128)S(1)}) custom-call(s32[2]{0:T(128)S(1)} %pad_add_fusion.meta, s32[32]{0:T(128)S(1)} %get-tuple-element.22.tab, s32[77]{0:T(128)S(1)} %get-tuple-element.28.lst, ...), custom_call_target="tpu_custom_call" | custom-call | flops 200000000 | bytes 8000000 | tf_op jit(solution)/shard_map/last/pallas_call | solution.py:586
  57.7 3.5 %all-to-all-done.3.got = f32[16,1,128]{2,1,0:T(1,128)S(1)} async-done(((f32[16,1,128]{2,1,0:T(1,128)}), f32[16,1,128]{2,1,0:T(1,128)S(1)}, u32[]{:S(2)}, u32[]{:S(2)}) %all-to-all-start.3) | async-done | bytes 8224 | tf_op jit(solution)/shard_map/all_to_all | solution.py:584
  61.2 0.8 %finish.1 = (f32[4,4,384]{2,1,0:T(4,128)}, f32[4,4,384]{2,1,0:T(4,128)}) custom-call(f32[8,128]{1,0:T(8,128)S(1)} %get-tuple-element.33.steps, f32[16,1,128]{2,1,0:T(1,128)S(1)} %all-to-all-done.3.got, f32[4,4,384]{2,1,0:T(4,128)S(1)} %get-tuple-element.37.o_p, f32[4,4,384]{2,1,0:T(4,128)S(1)} %get-tuple-element.38.o_z, ...), custom_call_target="tpu_custom_call" | custom-call | tf_op jit(solution)/shard_map/finish/pallas_call | solution.py:596
  (2 shorter events, 0.0 us)
Async XLA Ops:
  0.6 0.7 %copy-start.8 = (f32[4,128]{1,0:T(4,128)S(1)}, f32[4,128]{1,0:T(4,128)}, u32[]{:S(2)}) copy-start(f32[4,128]{1,0:T(4,128)} %resid.1) | copy-start | bytes 6148
  0.6 0.7 %copy-start.7 = (f32[4,128]{1,0:T(4,128)S(1)}, f32[4,128]{1,0:T(4,128)}, u32[]{:S(2)}) copy-start(f32[4,128]{1,0:T(4,128)} %weight.1) | copy-start | bytes 6148
  0.7 0.7 %copy-start.6 = (s32[4,128]{1,0:T(4,128)S(1)}, s32[4,128]{1,0:T(4,128)}, u32[]{:S(2)}) copy-start(s32[4,128]{1,0:T(4,128)} %match.1) | copy-start | bytes 6148
  0.7 0.7 %copy-start.5 = (s32[4,128]{1,0:T(4,128)S(1)}, s32[4,128]{1,0:T(4,128)}, u32[]{:S(2)}) copy-start(s32[4,128]{1,0:T(4,128)} %knot_par.1) | copy-start | bytes 6148
  0.7 0.7 %copy-start.4 = (s32[4,128]{1,0:T(4,128)S(1)}, s32[4,128]{1,0:T(4,128)}, u32[]{:S(2)}) copy-start(s32[4,128]{1,0:T(4,128)} %knot_own.1) | copy-start | bytes 6148
  0.7 0.7 %copy-start.3 = (s32[64,4]{0,1:T(4,128)S(1)}, s32[64,4]{0,1:T(4,128)}, u32[]{:S(2)}) copy-start(s32[64,4]{0,1:T(4,128)} %param.12) | copy-start | bytes 3076
  0.7 0.7 %copy-start.1 = (f32[2,4,128]{2,1,0:T(4,128)S(1)}, f32[2,4,128]{2,1,0:T(4,128)}, u32[]{:S(2)}) copy-start(f32[2,4,128]{2,1,0:T(4,128)} %spline.1) | copy-start | bytes 12292
  0.8 0.7 %copy-start.2 = (s32[64,4]{0,1:T(4,128)S(1)}, s32[64,4]{0,1:T(4,128)}, u32[]{:S(2)}) copy-start(s32[64,4]{0,1:T(4,128)} %param.11) | copy-start | bytes 3076
  0.8 0.7 %copy-start.9 = (s32[4]{0:T(128)S(1)}, s32[4]{0:T(128)}, u32[]{:S(2)}) copy-start(s32[4]{0:T(128)} %counts.1) | copy-start | bytes 52
  1.5 0.7 %copy-start = (f32[12,4,128]{2,1,0:T(4,128)S(1)}, f32[12,4,128]{2,1,0:T(4,128)}, u32[]{:S(2)}) copy-start(f32[12,4,128]{2,1,0:T(4,128)} %geometry.1) | copy-start | bytes 73732
  3.9 19.0 %all-to-all-start = ((f32[32,5,4,128]{3,2,1,0:T(4,128)}), f32[32,5,4,128]{3,2,1,0:T(4,128)S(1)}, u32[]{:S(2)}, u32[]{:S(2)}) async-start(f32[32,5,4,128]{3,2,1,0:T(4,128)} %bitcast.6), calls=%async_computation | async-start | bytes 655360 | tf_op jit(solution)/shard_map/all_to_all | solution.py:544
  11.2 5.1 %collective-permute-start = (f32[4,16,128]{2,1,0:T(8,128)S(1)}, f32[4,16,128]{2,1,0:T(8,128)S(1)}, u32[]{:S(2)}, u32[]{:S(2)}) collective-permute-start(f32[4,16,128]{2,1,0:T(8,128)S(1)} %get-tuple-element.23), channel_id=1, source_target_pairs={{0,1},{1,0},{2,3},{3,2},{4,5},{5,4},{6,7},{7,6},{8,9},{9,8},{10,11... | collective-permute-start | bytes 98312 | tf_op jit(solution)/shard_map/ppermute | solution.py:539
  51.4 9.8 %all-to-all-start.3 = ((f32[16,1,128]{2,1,0:T(1,128)}), f32[16,1,128]{2,1,0:T(1,128)S(1)}, u32[]{:S(2)}, u32[]{:S(2)}) async-start(f32[16,1,128]{2,1,0:T(1,128)} %get-tuple-element.34), calls=%async_computation.3 | async-start | bytes 16384 | tf_op jit(solution)/shard_map/all_to_all | solution.py:584

commit v4 on v3

--- a/solution.py
+++ b/solution.py
@@ -133,14 +133,15 @@
 
 
 def send_kernel(
-    meta, counts, dev, picks, knot_own, knot_par, match, spline, geometry, weight, resid,
+    counts, dev, picks, knot_own, knot_par, match, spline, geometry, weight, resid,
     send, own, tab, filled, taken, normals_s, knots_s, match_s,
 ):
     drives = counts.shape[0]
     lanes = send.shape[0]
     street_size = send.shape[1]
-    lane = meta[0]
-    street = meta[1]
+    lane = lax.axis_index("drive")
+    street = lax.axis_index("street")
+    tab[2 * drives * MATCH] = street
     for j in range(lanes):
         taken[j] = 0
         filled[2 * j] = -1
@@ -410,7 +411,7 @@
 
 
 def last_kernel(
-    meta, tab, lst, own, inc, direction, image, values, sent, got, sent2, got2, resid, precond,
+    tab, lst, own, inc, direction, image, values, sent, got, sent2, got2, resid, precond,
     steps, o_p, o_z, o_r, o_h, o_q, acc, hess,
 ):
     street_size, drives = own.shape[0], own.shape[1]
@@ -448,7 +449,7 @@
         points.append(point)
         masks.append(row == entry - point * DOF)
     for bl in range(blocks):
-        block = meta[1] * blocks + bl
+        block = tab[2 * entries] * blocks + bl
         high = jnp.right_shift(block, 1)
         offset = jnp.bitwise_and(block, 1) * (LANES // 2)
         indices = [offset + points[q] for q in range(tiles)]
@@ -481,7 +482,7 @@
         resid_out[a] = o_r[a] - last * (o_h[a] + beta * o_q[a])
 
 
-def call(kernel, shapes, spaces_in, spaces_out, scratch=(), **kwargs):
+def call(kernel, shapes, spaces_in, spaces_out, scratch=(), limit=40, **kwargs):
     where = {"s": pltpu.SMEM, "v": pltpu.VMEM}
     return pl.pallas_call(
         kernel,
@@ -489,7 +490,7 @@
         in_specs=[pl.BlockSpec(memory_space=where[c]) for c in spaces_in],
         out_specs=[pl.BlockSpec(memory_space=where[c]) for c in spaces_out],
         scratch_shapes=list(scratch),
-        compiler_params=pltpu.CompilerParams(vmem_limit_bytes=40 * 1024 * 1024),
+        compiler_params=pltpu.CompilerParams(vmem_limit_bytes=limit * 1024 * 1024),
         **kwargs,
     )
 
@@ -509,7 +510,6 @@
     drives = knot_own.shape[0]
     lanes = lax.axis_size("drive")
     street_size = lax.axis_size("street")
-    meta = jnp.stack([lax.axis_index("drive"), lax.axis_index("street")]).astype(jnp.int32)
     entries = drives * MATCH
     blocks = lanes * street_size
     param = ((drives, HIGH, SUB, LANES), F32)
@@ -522,9 +522,9 @@
         [
             ((lanes, street_size, 5, 4, LANES), F32),
             ((drives, 2 * SUB, LANES), F32),
-            ((2 * entries,), jnp.int32),
+            ((2 * entries + 1,), jnp.int32),
         ],
-        "ssssvvvvvvv",
+        "sssvvvvvvv",
         "vvs",
         [
             pltpu.SMEM((CAP * lanes,), jnp.int32),
@@ -534,10 +534,11 @@
             pltpu.VMEM((drives, SUB, LANES), jnp.int32),
         ],
         name="send",
-    )(meta, *arrays)
+        limit=60,
+    )(*arrays)
     if street_size == 2:
         peer = lax.ppermute(mine, "street", [(0, 1), (1, 0)])
-        first = meta[1] == 0
+        first = lax.axis_index("street") == 0
         own = jnp.stack([jnp.where(first, mine, peer), jnp.where(first, peer, mine)])
     else:
         own = lax.all_gather(mine, "street", axis=0, tiled=False)
@@ -586,12 +587,12 @@
     parts = call(
         last_kernel,
         [shape] * 5,
-        "sssvvvvvvvvvvvv",
+        "ssvvvvvvvvvvvv",
         "vvvvv",
         [acc, pltpu.VMEM(param[0], F32)],
         name="last",
         cost_estimate=pl.CostEstimate(flops=200000000, bytes_accessed=8000000, transcendentals=0),
-    )(meta, tab, lst, own, inc, direction, image, values, sent, got, sent2, got2, resid, precond, steps)
+    )(tab, lst, own, inc, direction, image, values, sent, got, sent2, got2, resid, precond, steps)
     return tuple(
         call(finish_kernel, [shape, shape], "vvvvvvv", "vv", name="finish")(steps, got3, *parts)
     )

time: 62.6 us -> 62 us (level); the launches traced: 62 us -> 62.3 us
  blocking collectives: 19.6 us -> 21.2 us
  local copies, waits for them, and re-layouts: 1.43 us -> 0.01 us
    unnamed x20 -> x4, local copies, waits for them, and re-layouts: 1.43 us -> 0.01 us
    all_to_all x1, blocking collectives: 10 us -> 11 us  [body(): got = lax.all_to_all(sent, 'drive', split_axis=0, concat_axis=0, tiled=True)]
where the time goes in v4:
time: 62 us; the launch traced here: 62.3 us
  blocking collectives  21.2 us (34%)
  Pallas kernels  15 us (24%)
  waiting for transfers between devices  12.8 us (21%)
  starting transfers between devices  12.6 us (20%)
  between operations  0.71 us (1%)
    all_to_all x1, blocking collectives, body(): got = lax.all_to_all(sent, 'drive', split_axis=0, concat_axis=0, tiled=True)  11 us
    all_to_all x1, blocking collectives, body(): lax.all_to_all(sent2, 'drive', split_axis=0, concat_axis=0, tiled=True)  10.1 us
    all_to_all x1, starting transfers between devices, body(): lax.all_to_all(send.reshape(blocks, 5, 4, LANES), ('drive', 'street'), sp...  7.3 us
    all_to_all x1, waiting for transfers between devices, body(): lax.all_to_all(send.reshape(blocks, 5, 4, LANES), ('drive', 'street'), sp...  6.09 us
    pallas_call x1, Pallas kernels, body(): call(start_kernel, [param, param, param, exchange, ((list_size,), jnp.int...  3.99 us
    pallas_call x1, Pallas kernels, body(): call(middle_kernel, [param, ((street_size * drives, LANES), F32), exchang...  3.53 us
    all_to_all x1, starting transfers between devices, body(): lax.all_to_all(sent3, 'drive', split_axis=0, concat_axis=0, tiled=True)  3.47 us
    all_to_all x1, waiting for transfers between devices, body(): lax.all_to_all(sent3, 'drive', split_axis=0, concat_axis=0, tiled=True)  3.44 us
  transfers between devices with their start and end apart: 3, of which 3 were waited for; matrix products, arithmetic and copies ran while one was open for 0% of the time, Pallas kernels for 5%

profile of v4, /device:TPU:0, one launch (start us, length us, event | category | flops | bytes accessed | tf_op | source)
XLA Modules:
  0.0 62.3 jit_solution(7134734199234302947)
XLA Ops:
  0.6 2.0 %send.1 = (f32[16,2,5,4,128]{4,3,2,1,0:T(4,128)}, f32[4,16,128]{2,1,0:T(8,128)}, s32[33]{0:T(128)}) custom-call(s32[4]{0:T(128)} %counts.1, s32[4,64]{1,0:T(4,128)} %bitcast.8, s32[4,64]{1,0:T(4,128)} %bitcast.9, s32[4,128]{1,0:T(4,128)} %knot_own.1, s32[4,128]{1,0:T(4,128)} %knot_par.1, s32[4,128]{1,0:T(4,128)} %match.1, f32[2,4,128]{2,1,0:T(4,128)} %spline.1, ...), custom_call_target="tpu_custom_call" | custom-call | tf_op jit(solution)/shard_map/send/pallas_call | solution.py:520
  2.6 0.0 copy-start.1
  2.6 7.3 %all-to-all-start = ((f32[32,5,4,128]{3,2,1,0:T(4,128)}), f32[32,5,4,128]{3,2,1,0:T(4,128)S(1)}, u32[]{:S(2)}, u32[]{:S(2)}) async-start(f32[32,5,4,128]{3,2,1,0:T(4,128)} %bitcast.7), calls=%async_computation | async-start | bytes 655360 | tf_op jit(solution)/shard_map/all_to_all | solution.py:545
  9.9 0.0 copy-done.1
  10.0 1.8 %collective-permute-start = (f32[4,16,128]{2,1,0:T(8,128)S(1)}, f32[4,16,128]{2,1,0:T(8,128)S(1)}, u32[]{:S(2)}, u32[]{:S(2)}) collective-permute-start(f32[4,16,128]{2,1,0:T(8,128)S(1)} %copy-done.1), channel_id=1, source_target_pairs={{0,1},{1,0},{2,3},{3,2},{4,5},{5,4},{6,7},{7,6},{8,9},{9,8},{10,11... | collective-permute-start | bytes 98312 | tf_op jit(solution)/shard_map/ppermute | solution.py:540
  11.8 3.3 %collective-permute-done = f32[4,16,128]{2,1,0:T(8,128)S(1)} collective-permute-done((f32[4,16,128]{2,1,0:T(8,128)S(1)}, f32[4,16,128]{2,1,0:T(8,128)S(1)}, u32[]{:S(2)}, u32[]{:S(2)}) %collective-permute-start) | collective-permute-done | bytes 32800 | tf_op jit(solution)/shard_map/ppermute | solution.py:540
  15.1 0.4 own.1.begun
  15.6 0.0 copy-start
  15.6 6.1 %all-to-all-done.inc = f32[32,5,4,128]{3,2,1,0:T(4,128)S(1)} async-done(((f32[32,5,4,128]{3,2,1,0:T(4,128)}), f32[32,5,4,128]{3,2,1,0:T(4,128)S(1)}, u32[]{:S(2)}, u32[]{:S(2)}) %all-to-all-start) | async-done | bytes 327712 | tf_op jit(solution)/shard_map/all_to_all | solution.py:545
  21.7 0.0 copy-done
  21.7 4.0 %start.1 = (f32[4,4,8,128]{3,2,1,0:T(8,128)S(1)}, f32[4,4,8,128]{3,2,1,0:T(8,128)S(1)}, f32[4,4,8,128]{3,2,1,0:T(8,128)S(1)}, f32[16,8,1,128]{3,2,1,0:T(1,128)S(1)}, s32[77]{0:T(128)S(1)}) custom-call(s32[33]{0:T(128)S(1)} %copy-done, f32[2,4,16,128]{3,2,1,0:T(8,128)S(1)} %pad_maximum_fusion.own, f32[32,5,4,128]{3,2,1,0:T(4,128)S(1)} %all-to-all-done.inc, ...), custom_call_target="tpu_custom_call" | custom-call | tf_op jit(solution)/shard_map/start/pallas_call | solution.py:560
  25.7 11.0 %all_to_all.20.got = f32[16,8,1,128]{3,2,1,0:T(1,128)S(1)} all-to-all(f32[16,8,1,128]{3,2,1,0:T(1,128)S(1)} %get-tuple-element.29.sent), channel_id=1, replica_groups=mesh['region'=1,'drive'=16,'street'=2] {'drive'}, dimensions={0} | all-to-all | bytes 131072 | tf_op jit(solution)/shard_map/all_to_all | solution.py:568
  36.7 3.5 %middle.1 = (f32[4,4,8,128]{3,2,1,0:T(8,128)S(1)}, f32[8,128]{1,0:T(8,128)S(1)}, f32[16,9,1,128]{3,2,1,0:T(1,128)S(1)}) custom-call(s32[33]{0:T(128)S(1)} %copy-done, s32[77]{0:T(128)S(1)} %get-tuple-element.28.lst, f32[2,4,16,128]{3,2,1,0:T(8,128)S(1)} %pad_maximum_fusion.own, f32[32,5,4,128]{3,2,1,0:T(4,128)S(1)} %all-to-all-done.inc, ...), custom_call_target="tpu_custom_call" | custom-call | tf_op jit(solution)/shard_map/middle/pallas_call | solution.py:569
  40.2 10.1 %all_to_all.21.got.got2 = f32[16,9,1,128]{3,2,1,0:T(1,128)S(1)} all-to-all(f32[16,9,1,128]{3,2,1,0:T(1,128)S(1)} %get-tuple-element.32.sent.sent2), channel_id=1, replica_groups=mesh['region'=1,'drive'=16,'street'=2] {'drive'}, dimensions={0} | all-to-all | bytes 147456 | tf_op jit(solution)/shard_map/all_to_all | solution.py:577
  50.4 1.4 %dots.1 = (f32[4,4,8,128]{3,2,1,0:T(8,128)S(1)}, f32[4,4,8,128]{3,2,1,0:T(8,128)S(1)}, f32[8,128]{1,0:T(8,128)S(1)}, f32[16,1,128]{2,1,0:T(1,128)}) custom-call(s32[33]{0:T(128)S(1)} %copy-done, f32[4,4,8,128]{3,2,1,0:T(8,128)S(1)} %get-tuple-element.25.grad, f32[4,4,8,128]{3,2,1,0:T(8,128)S(1)} %get-tuple-element.26.diag, ...), custom_call_target="tpu_custom_call" | custom-call | tf_op jit(solution)/shard_map/dots/pallas_call | solution.py:578
  51.7 3.5 %all-to-all-start.3 = ((f32[16,1,128]{2,1,0:T(1,128)}), f32[16,1,128]{2,1,0:T(1,128)S(1)}, u32[]{:S(2)}, u32[]{:S(2)}) async-start(f32[16,1,128]{2,1,0:T(1,128)} %get-tuple-element.34), calls=%async_computation.3 | async-start | bytes 16384 | tf_op jit(solution)/shard_map/all_to_all | solution.py:585
  55.2 2.9 %last.1 = (f32[4,4,384]{2,1,0:T(4,128)S(1)}, f32[4,4,384]{2,1,0:T(4,128)S(1)}, f32[4,4,384]{2,1,0:T(4,128)S(1)}, f32[4,4,384]{2,1,0:T(4,128)S(1)}, f32[4,4,384]{2,1,0:T(4,128)S(1)}) custom-call(s32[33]{0:T(128)S(1)} %copy-done, s32[77]{0:T(128)S(1)} %get-tuple-element.28.lst, f32[2,4,16,128]{3,2,1,0:T(8,128)S(1)} %pad_maximum_fusion.own, ...), custom_call_target="tpu_custom_call" | custom-call | flops 200000000 | bytes 8000000 | tf_op jit(solution)/shard_map/last/pallas_call | solution.py:587
  58.1 3.4 %all-to-all-done.3.got = f32[16,1,128]{2,1,0:T(1,128)S(1)} async-done(((f32[16,1,128]{2,1,0:T(1,128)}), f32[16,1,128]{2,1,0:T(1,128)S(1)}, u32[]{:S(2)}, u32[]{:S(2)}) %all-to-all-start.3) | async-done | bytes 8224 | tf_op jit(solution)/shard_map/all_to_all | solution.py:585
  61.5 0.8 %finish.1 = (f32[4,4,384]{2,1,0:T(4,128)}, f32[4,4,384]{2,1,0:T(4,128)}) custom-call(f32[8,128]{1,0:T(8,128)S(1)} %get-tuple-element.33.steps, f32[16,1,128]{2,1,0:T(1,128)S(1)} %all-to-all-done.3.got, f32[4,4,384]{2,1,0:T(4,128)S(1)} %get-tuple-element.37.o_p, f32[4,4,384]{2,1,0:T(4,128)S(1)} %get-tuple-element.38.o_z, ...), custom_call_target="tpu_custom_call" | custom-call | tf_op jit(solution)/shard_map/finish/pallas_call | solution.py:597
  (2 shorter events, 0.0 us)
Async XLA Ops:
  2.6 7.3 %copy-start.1 = (f32[4,16,128]{2,1,0:T(8,128)S(1)}, f32[4,16,128]{2,1,0:T(8,128)}, u32[]{:S(2)}) copy-start(f32[4,16,128]{2,1,0:T(8,128)} %get-tuple-element.23) | copy-start | bytes 98308
  2.6 19.0 %all-to-all-start = ((f32[32,5,4,128]{3,2,1,0:T(4,128)}), f32[32,5,4,128]{3,2,1,0:T(4,128)S(1)}, u32[]{:S(2)}, u32[]{:S(2)}) async-start(f32[32,5,4,128]{3,2,1,0:T(4,128)} %bitcast.7), calls=%async_computation | async-start | bytes 655360 | tf_op jit(solution)/shard_map/all_to_all | solution.py:545
  10.0 5.1 %collective-permute-start = (f32[4,16,128]{2,1,0:T(8,128)S(1)}, f32[4,16,128]{2,1,0:T(8,128)S(1)}, u32[]{:S(2)}, u32[]{:S(2)}) collective-permute-start(f32[4,16,128]{2,1,0:T(8,128)S(1)} %copy-done.1), channel_id=1, source_target_pairs={{0,1},{1,0},{2,3},{3,2},{4,5},{5,4},{6,7},{7,6},{8,9},{9,8},{10,11... | collective-permute-start | bytes 98312 | tf_op jit(solution)/shard_map/ppermute | solution.py:540
  15.6 6.1 %copy-start = (s32[33]{0:T(128)S(1)}, s32[33]{0:T(128)}, u32[]{:S(2)}) copy-start(s32[33]{0:T(128)} %get-tuple-element.22.tab) | copy-start | bytes 400
  51.7 9.8 %all-to-all-start.3 = ((f32[16,1,128]{2,1,0:T(1,128)}), f32[16,1,128]{2,1,0:T(1,128)S(1)}, u32[]{:S(2)}, u32[]{:S(2)}) async-start(f32[16,1,128]{2,1,0:T(1,128)} %get-tuple-element.34), calls=%async_computation.3 | async-start | bytes 16384 | tf_op jit(solution)/shard_map/all_to_all | solution.py:585

commit v5 on v4

--- a/solution.py
+++ b/solution.py
@@ -91,15 +91,26 @@
     return out
 
 
-def gather_value(tiles, knot, basis, normals):
+def shift_tiles(shifted, tiles_ref):
+    lane = iota((SUB, LANES), 1)
+    for a in range(tiles_ref.shape[0]):
+        tiles = [tiles_ref[a, h] for h in range(HIGH)]
+        for k in range(4):
+            rolled = [pltpu.roll(t, LANES - k, axis=1) for t in tiles] if k else tiles
+            for h in range(HIGH):
+                after = rolled[min(h + 1, HIGH - 1)]
+                shifted[a, k, h] = jnp.where(lane < LANES - k, rolled[h], after) if k else rolled[h]
+
+
+def gather_value(shifted, drive, knot, basis, normals):
+    low = jnp.bitwise_and(knot, LANES - 1)
+    high = jnp.right_shift(knot, 7)
+    here = [high == h for h in range(HIGH - 1)]
     total = None
     for k in range(4):
-        index = knot + k
-        low = jnp.bitwise_and(index, LANES - 1)
-        high = jnp.right_shift(index, 7)
-        value = take_lanes(tiles[HIGH - 1], low)
+        value = take_lanes(shifted[drive, k, HIGH - 1], low)
         for h in range(HIGH - 1):
-            value = jnp.where(high == h, take_lanes(tiles[h], low), value)
+            value = jnp.where(here[h], take_lanes(shifted[drive, k, h], low), value)
         term = basis[k] * value
         total = term if total is None else total + term
     return jnp.sum(normals * total, axis=0, keepdims=True)
@@ -134,27 +145,26 @@
 
 def send_kernel(
     counts, dev, picks, knot_own, knot_par, match, spline, geometry, weight, resid,
-    send, own, tab, filled, taken, normals_s, knots_s, match_s,
+    send, own, tab,
 ):
     drives = counts.shape[0]
-    lanes = send.shape[0]
     street_size = send.shape[1]
     lane = lax.axis_index("drive")
     street = lax.axis_index("street")
     tab[2 * drives * MATCH] = street
-    for j in range(lanes):
-        taken[j] = 0
-        filled[2 * j] = -1
-        filled[2 * j + 1] = -1
-    for a in range(drives):
-        for m in range(MATCH):
-            e = a * MATCH + m
-            dest = dev[m, lane * drives + a]
-            rank = taken[dest]
-            taken[dest] = rank + 1
-            tab[e] = dest
-            tab[drives * MATCH + e] = rank
-            filled[2 * dest + rank] = e
+    entries = drives * MATCH
+    dests = [dev[e % MATCH, lane * drives + e // MATCH] for e in range(entries)]
+    ranks = []
+    for e in range(entries):
+        rank = 0
+        for other in range(e // MATCH * MATCH):
+            rank = rank + jnp.where(dests[other] == dests[e], 1, 0)
+        ranks.append(rank)
+        tab[e] = dests[e]
+        tab[entries + e] = rank
+    for j in range(send.shape[0]):
+        for t in range(street_size):
+            send[j, t, 4] = jnp.zeros((4, LANES), F32)
     slot = street * LANES + iota((1, LANES), 1)
     zero1 = jnp.zeros((1, LANES), F32)
     for a in range(drives):
@@ -167,53 +177,46 @@
         own[a, SUB : 2 * SUB, :] = jnp.concatenate(
             [knot_own[a : a + 1, :].astype(F32), spline[0, a : a + 1, :], rho] + [zero1] * 5, axis=0
         )
-        normals_s[a] = jnp.concatenate(
+        tile = jnp.concatenate(
             [-(geometry[DOF + d, a : a + 1, :] * root) for d in range(DOF)]
             + [spline[1, a : a + 1, :], rho],
             axis=0,
         )
-        knots_s[a] = jnp.broadcast_to(knot_par[a : a + 1, :].astype(F32), (4, LANES))
-        match_s[a] = jnp.broadcast_to(match[a : a + 1, :], (SUB, LANES))
-    row = iota((4, LANES), 0)
-    for j in range(lanes):
-        normals = []
-        infos = []
-        flags = []
-        for r in range(CAP):
-            e = filled[2 * j + r]
-            safe = jnp.maximum(e, 0)
-            a = jnp.right_shift(safe, 2)
-            m = jnp.where(e < 0, -1, jnp.bitwise_and(safe, 3))
-            pick = picks[jnp.bitwise_and(safe, 3), lane * drives + a]
-            there = jnp.logical_and(e >= 0, counts[a] > street * LANES)
-            flags.append(jnp.where(there, pick + 1, 0).astype(F32))
-            normals.append(jnp.where(match_s[a] == m, normals_s[a], 0.0))
-            infos.append(knots_s[a])
-        info = jnp.where(row == 0, infos[0], infos[1])
-        info = jnp.where(row == 2, flags[0], jnp.where(row == 3, flags[1], info))
-        for t in range(street_size):
-            for r in range(CAP):
-                send[j, t, 2 * r] = normals[r][0:4]
-                send[j, t, 2 * r + 1] = normals[r][4:8]
-            send[j, t, 4] = info
-
-
-def put_values(out_ref, tab, own_ref, inc_ref, lst, tiles_ref):
+        knots = knot_par[a : a + 1, :].astype(F32)
+        matches = jnp.broadcast_to(match[a : a + 1, :], (SUB, LANES))
+        some_live = counts[a] > street * LANES
+        for m in range(MATCH):
+            e = a * MATCH + m
+            flag = jnp.where(some_live, picks[m, lane * drives + a] + 1, 0).astype(F32)
+            normals = jnp.where(matches == m, tile, 0.0)
+            flags = jnp.full((1, LANES), flag, F32)
+            for t in range(street_size):
+                for half in range(2):
+                    send[dests[e], t, 2 * ranks[e] + half] = normals[4 * half : 4 * half + 4]
+                send[dests[e], t, 4, pl.ds(ranks[e], 1), :] = knots
+                send[dests[e], t, 4, pl.ds(CAP + ranks[e], 1), :] = flags
+
+
+def read_places(tab, street_size, entries):
+    return [(tab[e], tab[entries + e] * street_size) for e in range(entries)]
+
+
+def put_values(out_ref, tab, own_ref, inc_ref, lst, tiles_ref, shifted):
     street_size, drives = own_ref.shape[0], own_ref.shape[1]
-    entries = drives * MATCH
-    for a in range(drives):
-        tiles = [tiles_ref[a, h] for h in range(HIGH)]
+    at = read_places(tab, street_size, drives * MATCH)
+    shift_tiles(shifted, tiles_ref)
+    for a in range(drives):
         for s in range(street_size):
             normals, knot, basis, _ = own_tile(own_ref, s, a)
-            value = gather_value(tiles, knot, basis, normals)
+            value = gather_value(shifted, a, knot, basis, normals)
             for m in range(MATCH):
-                e = a * MATCH + m
-                out_ref[tab[e], tab[entries + e] * street_size + s] = value
+                lane, first = at[a * MATCH + m]
+                out_ref[lane, first + s] = value
 
     def one(code):
         pick, rank, block, lane, part = decode(code, street_size)
         normals, knot, basis, _ = inc_tile(inc_ref, block, rank)
-        value = gather_value([tiles_ref[pick, h] for h in range(HIGH)], knot, basis, normals)
+        value = gather_value(shifted, pick, knot, basis, normals)
         out_ref[lane, (CAP + rank) * street_size + part] = value
 
     count = lst[lst.shape[0] - 1]
@@ -226,12 +229,11 @@
     lax.fori_loop(0, lax.div(count + UNROLL - 1, UNROLL), some, 0)
 
 
-def own_sum(sent, got, tab, a, s, street_size, entries):
-    e = a * MATCH
-    total = sent[tab[e], tab[entries + e] * street_size + s]
-    for m in range(MATCH):
-        e = a * MATCH + m
-        total = total + got[tab[e], (CAP + tab[entries + e]) * street_size + s]
+def own_sum(sent, got, at, a, s, street_size):
+    lane, first = at[a * MATCH]
+    total = sent[lane, first + s]
+    for lane, first in at[a * MATCH : (a + 1) * MATCH]:
+        total = total + got[lane, first + CAP * street_size + s]
     return total
 
 
@@ -282,7 +284,7 @@
     spread_own(acc, own, start_kinds)
 
 
-def start_kernel(tab, own, inc, begun, grad, diag, direction, out, lst, acc):
+def start_kernel(tab, own, inc, begun, grad, diag, direction, out, lst, acc, shifted):
     drives = own.shape[1]
     street_size = own.shape[0]
     blocks = inc.shape[0]
@@ -314,7 +316,7 @@
             diag[a, h] = diagonal
             direction[a, h] = gradient[h] / diagonal
     out[...] = jnp.zeros(out.shape, F32)
-    put_values(out, tab, own, inc, lst, direction)
+    put_values(out, tab, own, inc, lst, direction, shifted)
 
 
 def scalar_row(values):
@@ -331,13 +333,13 @@
 
 
 def middle_kernel(
-    tab, lst, own, inc, grad, diag, direction, sent, got, image, values, out, acc, ratio
+    tab, lst, own, inc, grad, diag, direction, sent, got, image, values, out, acc, ratio, shifted
 ):
     street_size, drives = own.shape[0], own.shape[1]
-    entries = drives * MATCH
+    at = read_places(tab, street_size, drives * MATCH)
     for a in range(drives):
         for s in range(street_size):
-            values[pl.ds(s * drives + a, 1), :] = own_sum(sent, got, tab, a, s, street_size, entries)
+            values[pl.ds(s * drives + a, 1), :] = own_sum(sent, got, at, a, s, street_size)
 
     def kinds_own(coeffs, rho, a, s):
         value = jnp.broadcast_to(values[pl.ds(s * drives + a, 1), :], (SUB, LANES))
@@ -362,7 +364,7 @@
             first = first + grad[a, h] * p
             second = second + p * q
     out[...] = jnp.zeros(out.shape, F32)
-    put_values(out, tab, own, inc, lst, ratio)
+    put_values(out, tab, own, inc, lst, ratio, shifted)
     row = scalar_row([first, second])
     rows = 2 * CAP * street_size
     for j in range(out.shape[0]):
@@ -372,7 +374,7 @@
 def dots_kernel(tab, grad, diag, direction, image, values, sent, got, resid, precond, steps, out):
     drives = grad.shape[0]
     street_size = values.shape[0] // drives
-    entries = drives * MATCH
+    at = read_places(tab, street_size, drives * MATCH)
     rows = 2 * CAP * street_size
     total = got[0, rows]
     for j in range(1, got.shape[0]):
@@ -397,7 +399,7 @@
     for a in range(drives):
         for s in range(street_size):
             before = values[pl.ds(s * drives + a, 1), :]
-            value = before - alpha * own_sum(sent, got, tab, a, s, street_size, entries)
+            value = before - alpha * own_sum(sent, got, at, a, s, street_size)
             slots2 = slots2 + value * value
             slots3 = slots3 + value * before
     head = iota((SUB, LANES), 0) == 0
@@ -416,11 +418,12 @@
 ):
     street_size, drives = own.shape[0], own.shape[1]
     entries = drives * MATCH
+    at = read_places(tab, street_size, entries)
     alpha = steps[0:1, 0:1]
 
     def kinds_own(coeffs, rho, a, s):
         value = values[pl.ds(s * drives + a, 1), :] - alpha * own_sum(
-            sent2, got2, tab, a, s, street_size, entries
+            sent2, got2, at, a, s, street_size
         )
         value = jnp.broadcast_to(value, (SUB, LANES))
         return [[c * value for c in coeffs]]
@@ -526,13 +529,6 @@
         ],
         "sssvvvvvvv",
         "vvs",
-        [
-            pltpu.SMEM((CAP * lanes,), jnp.int32),
-            pltpu.SMEM((lanes,), jnp.int32),
-            pltpu.VMEM((drives, SUB, LANES), F32),
-            pltpu.VMEM((drives, 4, LANES), F32),
-            pltpu.VMEM((drives, SUB, LANES), jnp.int32),
-        ],
         name="send",
         limit=60,
     )(*arrays)
@@ -548,6 +544,7 @@
     exchange = ((lanes, 2 * CAP * street_size, 1, LANES), F32)
     exchange2 = ((lanes, 2 * CAP * street_size + 1, 1, LANES), F32)
     acc = pltpu.VMEM((drives, 128, LANES), F32)
+    shifted = pltpu.VMEM((drives, 4, HIGH, SUB, LANES), F32)
     list_size = CAP * blocks + UNROLL
     (begun,) = call(
         own_kernel,
@@ -562,7 +559,7 @@
         [param, param, param, exchange, ((list_size,), jnp.int32)],
         "svvv",
         "vvvvs",
-        [pltpu.VMEM((drives, 256, LANES), F32)],
+        [pltpu.VMEM((drives, 256, LANES), F32), shifted],
         name="start",
     )(tab, own, inc, begun)
     got = lax.all_to_all(sent, "drive", split_axis=0, concat_axis=0, tiled=True)
@@ -571,7 +568,7 @@
         [param, ((street_size * drives, LANES), F32), exchange2],
         "ssvvvvvvv",
         "vvv",
-        [acc, pltpu.VMEM(param[0], F32)],
+        [acc, pltpu.VMEM(param[0], F32), shifted],
         name="middle",
     )(tab, lst, own, inc, grad, diag, direction, sent, got)
     got2 = lax.all_to_all(sent2, "drive", split_axis=0, concat_axis=0, tiled=True)

time: 62 us -> 60.6 us (0.977)
  blocking collectives: 21.2 us -> 20 us
  Pallas kernels: 15 us -> 14.3 us
    all_to_all x1, blocking collectives: 11 us -> 10.4 us  [body(): got = lax.all_to_all(sent, 'drive', split_axis=0, concat_axis=0, tiled=True)]
where the time goes in v5:
time: 60.6 us; the launch traced here: 60.5 us
  blocking collectives  20 us (33%)
  Pallas kernels  14.3 us (24%)
  waiting for transfers between devices  12.9 us (21%)
  starting transfers between devices  12.6 us (21%)
  between operations  0.71 us (1%)
    all_to_all x1, blocking collectives, body(): got = lax.all_to_all(sent, 'drive', split_axis=0, concat_axis=0, tiled=True)  10.4 us
    all_to_all x1, blocking collectives, body(): lax.all_to_all(sent2, 'drive', split_axis=0, concat_axis=0, tiled=True)  9.6 us
    all_to_all x1, starting transfers between devices, body(): lax.all_to_all(send.reshape(blocks, 5, 4, LANES), ('drive', 'street'), sp...  7.3 us
    all_to_all x1, waiting for transfers between devices, body(): lax.all_to_all(send.reshape(blocks, 5, 4, LANES), ('drive', 'street'), sp...  6.09 us
    pallas_call x1, Pallas kernels, body(): call(start_kernel, [param, param, param, exchange, ((list_size,), jnp.int...  3.75 us
    all_to_all x1, starting transfers between devices, body(): lax.all_to_all(sent3, 'drive', split_axis=0, concat_axis=0, tiled=True)  3.47 us
    all_to_all x1, waiting for transfers between devices, body(): lax.all_to_all(sent3, 'drive', split_axis=0, concat_axis=0, tiled=True)  3.47 us
    ppermute x1, waiting for transfers between devices, body(): peer = lax.ppermute(mine, 'street', [(0, 1), (1, 0)])  3.3 us
  transfers between devices with their start and end apart: 3, of which 3 were waited for; matrix products, arithmetic and copies ran while one was open for 0% of the time, Pallas kernels for 5%

profile of v5, /device:TPU:0, one launch (start us, length us, event | category | flops | bytes accessed | tf_op | source)
XLA Modules:
  0.0 60.5 jit_solution(12798942410575427977)
XLA Ops:
  0.6 1.9 %send.1 = (f32[16,2,5,4,128]{4,3,2,1,0:T(4,128)}, f32[4,16,128]{2,1,0:T(8,128)}, s32[33]{0:T(128)}) custom-call(s32[4]{0:T(128)} %counts.1, s32[4,64]{1,0:T(4,128)} %bitcast.8, s32[4,64]{1,0:T(4,128)} %bitcast.9, s32[4,128]{1,0:T(4,128)} %knot_own.1, s32[4,128]{1,0:T(4,128)} %knot_par.1, s32[4,128]{1,0:T(4,128)} %match.1, f32[2,4,128]{2,1,0:T(4,128)} %spline.1, ...), custom_call_target="tpu_custom_call" | custom-call | tf_op jit(solution)/shard_map/send/pallas_call | solution.py:523
  2.5 0.0 copy-start.1
  2.5 7.3 %all-to-all-start = ((f32[32,5,4,128]{3,2,1,0:T(4,128)}), f32[32,5,4,128]{3,2,1,0:T(4,128)S(1)}, u32[]{:S(2)}, u32[]{:S(2)}) async-start(f32[32,5,4,128]{3,2,1,0:T(4,128)} %bitcast.7), calls=%async_computation | async-start | bytes 655360 | tf_op jit(solution)/shard_map/all_to_all | solution.py:541
  9.8 0.0 copy-done.1
  9.8 1.8 %collective-permute-start = (f32[4,16,128]{2,1,0:T(8,128)S(1)}, f32[4,16,128]{2,1,0:T(8,128)S(1)}, u32[]{:S(2)}, u32[]{:S(2)}) collective-permute-start(f32[4,16,128]{2,1,0:T(8,128)S(1)} %copy-done.1), channel_id=1, source_target_pairs={{0,1},{1,0},{2,3},{3,2},{4,5},{5,4},{6,7},{7,6},{8,9},{9,8},{10,11... | collective-permute-start | bytes 98312 | tf_op jit(solution)/shard_map/ppermute | solution.py:536
  11.7 3.3 %collective-permute-done = f32[4,16,128]{2,1,0:T(8,128)S(1)} collective-permute-done((f32[4,16,128]{2,1,0:T(8,128)S(1)}, f32[4,16,128]{2,1,0:T(8,128)S(1)}, u32[]{:S(2)}, u32[]{:S(2)}) %collective-permute-start) | collective-permute-done | bytes 32800 | tf_op jit(solution)/shard_map/ppermute | solution.py:536
  15.0 0.4 own.1.begun
  15.4 0.0 copy-start
  15.4 6.1 %all-to-all-done.inc = f32[32,5,4,128]{3,2,1,0:T(4,128)S(1)} async-done(((f32[32,5,4,128]{3,2,1,0:T(4,128)}), f32[32,5,4,128]{3,2,1,0:T(4,128)S(1)}, u32[]{:S(2)}, u32[]{:S(2)}) %all-to-all-start) | async-done | bytes 327712 | tf_op jit(solution)/shard_map/all_to_all | solution.py:541
  21.5 0.0 copy-done
  21.5 3.7 %start.1 = (f32[4,4,8,128]{3,2,1,0:T(8,128)S(1)}, f32[4,4,8,128]{3,2,1,0:T(8,128)S(1)}, f32[4,4,8,128]{3,2,1,0:T(8,128)S(1)}, f32[16,8,1,128]{3,2,1,0:T(1,128)S(1)}, s32[77]{0:T(128)S(1)}) custom-call(s32[33]{0:T(128)S(1)} %copy-done, f32[2,4,16,128]{3,2,1,0:T(8,128)S(1)} %pad_maximum_fusion.own, f32[32,5,4,128]{3,2,1,0:T(4,128)S(1)} %all-to-all-done.inc, ...), custom_call_target="tpu_custom_call" | custom-call | tf_op jit(solution)/shard_map/start/pallas_call | solution.py:557
  25.3 10.4 %all_to_all.20.got = f32[16,8,1,128]{3,2,1,0:T(1,128)S(1)} all-to-all(f32[16,8,1,128]{3,2,1,0:T(1,128)S(1)} %get-tuple-element.29.sent), channel_id=1, replica_groups=mesh['region'=1,'drive'=16,'street'=2] {'drive'}, dimensions={0} | all-to-all | bytes 131072 | tf_op jit(solution)/shard_map/all_to_all | solution.py:565
  35.7 3.2 %middle.1 = (f32[4,4,8,128]{3,2,1,0:T(8,128)S(1)}, f32[8,128]{1,0:T(8,128)S(1)}, f32[16,9,1,128]{3,2,1,0:T(1,128)S(1)}) custom-call(s32[33]{0:T(128)S(1)} %copy-done, s32[77]{0:T(128)S(1)} %get-tuple-element.28.lst, f32[2,4,16,128]{3,2,1,0:T(8,128)S(1)} %pad_maximum_fusion.own, f32[32,5,4,128]{3,2,1,0:T(4,128)S(1)} %all-to-all-done.inc, ...), custom_call_target="tpu_custom_call" | custom-call | tf_op jit(solution)/shard_map/middle/pallas_call | solution.py:566
  38.9 9.6 %all_to_all.21.got.got2 = f32[16,9,1,128]{3,2,1,0:T(1,128)S(1)} all-to-all(f32[16,9,1,128]{3,2,1,0:T(1,128)S(1)} %get-tuple-element.32.sent.sent2), channel_id=1, replica_groups=mesh['region'=1,'drive'=16,'street'=2] {'drive'}, dimensions={0} | all-to-all | bytes 147456 | tf_op jit(solution)/shard_map/all_to_all | solution.py:574
  48.5 1.4 %dots.1 = (f32[4,4,8,128]{3,2,1,0:T(8,128)S(1)}, f32[4,4,8,128]{3,2,1,0:T(8,128)S(1)}, f32[8,128]{1,0:T(8,128)S(1)}, f32[16,1,128]{2,1,0:T(1,128)}) custom-call(s32[33]{0:T(128)S(1)} %copy-done, f32[4,4,8,128]{3,2,1,0:T(8,128)S(1)} %get-tuple-element.25.grad, f32[4,4,8,128]{3,2,1,0:T(8,128)S(1)} %get-tuple-element.26.diag, ...), custom_call_target="tpu_custom_call" | custom-call | tf_op jit(solution)/shard_map/dots/pallas_call | solution.py:575
  49.9 3.5 %all-to-all-start.3 = ((f32[16,1,128]{2,1,0:T(1,128)}), f32[16,1,128]{2,1,0:T(1,128)S(1)}, u32[]{:S(2)}, u32[]{:S(2)}) async-start(f32[16,1,128]{2,1,0:T(1,128)} %get-tuple-element.34), calls=%async_computation.3 | async-start | bytes 16384 | tf_op jit(solution)/shard_map/all_to_all | solution.py:582
  53.3 2.8 %last.1 = (f32[4,4,384]{2,1,0:T(4,128)S(1)}, f32[4,4,384]{2,1,0:T(4,128)S(1)}, f32[4,4,384]{2,1,0:T(4,128)S(1)}, f32[4,4,384]{2,1,0:T(4,128)S(1)}, f32[4,4,384]{2,1,0:T(4,128)S(1)}) custom-call(s32[33]{0:T(128)S(1)} %copy-done, s32[77]{0:T(128)S(1)} %get-tuple-element.28.lst, f32[2,4,16,128]{3,2,1,0:T(8,128)S(1)} %pad_maximum_fusion.own, ...), custom_call_target="tpu_custom_call" | custom-call | flops 200000000 | bytes 8000000 | tf_op jit(solution)/shard_map/last/pallas_call | solution.py:584
  56.2 3.5 %all-to-all-done.3.got = f32[16,1,128]{2,1,0:T(1,128)S(1)} async-done(((f32[16,1,128]{2,1,0:T(1,128)}), f32[16,1,128]{2,1,0:T(1,128)S(1)}, u32[]{:S(2)}, u32[]{:S(2)}) %all-to-all-start.3) | async-done | bytes 8224 | tf_op jit(solution)/shard_map/all_to_all | solution.py:582
  59.6 0.8 %finish.1 = (f32[4,4,384]{2,1,0:T(4,128)}, f32[4,4,384]{2,1,0:T(4,128)}) custom-call(f32[8,128]{1,0:T(8,128)S(1)} %get-tuple-element.33.steps, f32[16,1,128]{2,1,0:T(1,128)S(1)} %all-to-all-done.3.got, f32[4,4,384]{2,1,0:T(4,128)S(1)} %get-tuple-element.37.o_p, f32[4,4,384]{2,1,0:T(4,128)S(1)} %get-tuple-element.38.o_z, ...), custom_call_target="tpu_custom_call" | custom-call | tf_op jit(solution)/shard_map/finish/pallas_call | solution.py:594
  (2 shorter events, 0.0 us)
Async XLA Ops:
  2.5 7.3 %copy-start.1 = (f32[4,16,128]{2,1,0:T(8,128)S(1)}, f32[4,16,128]{2,1,0:T(8,128)}, u32[]{:S(2)}) copy-start(f32[4,16,128]{2,1,0:T(8,128)} %get-tuple-element.23) | copy-start | bytes 98308
  2.5 19.0 %all-to-all-start = ((f32[32,5,4,128]{3,2,1,0:T(4,128)}), f32[32,5,4,128]{3,2,1,0:T(4,128)S(1)}, u32[]{:S(2)}, u32[]{:S(2)}) async-start(f32[32,5,4,128]{3,2,1,0:T(4,128)} %bitcast.7), calls=%async_computation | async-start | bytes 655360 | tf_op jit(solution)/shard_map/all_to_all | solution.py:541
  9.8 5.1 %collective-permute-start = (f32[4,16,128]{2,1,0:T(8,128)S(1)}, f32[4,16,128]{2,1,0:T(8,128)S(1)}, u32[]{:S(2)}, u32[]{:S(2)}) collective-permute-start(f32[4,16,128]{2,1,0:T(8,128)S(1)} %copy-done.1), channel_id=1, source_target_pairs={{0,1},{1,0},{2,3},{3,2},{4,5},{5,4},{6,7},{7,6},{8,9},{9,8},{10,11... | collective-permute-start | bytes 98312 | tf_op jit(solution)/shard_map/ppermute | solution.py:536
  15.4 6.1 %copy-start = (s32[33]{0:T(128)S(1)}, s32[33]{0:T(128)}, u32[]{:S(2)}) copy-start(s32[33]{0:T(128)} %get-tuple-element.22.tab) | copy-start | bytes 400
  49.9 9.8 %all-to-all-start.3 = ((f32[16,1,128]{2,1,0:T(1,128)}), f32[16,1,128]{2,1,0:T(1,128)S(1)}, u32[]{:S(2)}, u32[]{:S(2)}) async-start(f32[16,1,128]{2,1,0:T(1,128)} %get-tuple-element.34), calls=%async_computation.3 | async-start | bytes 16384 | tf_op jit(solution)/shard_map/all_to_all | solution.py:582

commit v6 on v5

--- a/solution.py
+++ b/solution.py
@@ -319,17 +319,10 @@
     put_values(out, tab, own, inc, lst, direction, shifted)
 
 
-def scalar_row(values):
-    lane = iota((1, LANES), 1)
-    row = jnp.zeros((1, LANES), F32)
-    for i, value in enumerate(values):
-        total = jnp.sum(jnp.sum(value, axis=0, keepdims=True), axis=1, keepdims=True)
-        row = jnp.where(lane == i, total, row)
-    return row
-
-
-def pick_lane(row, i):
-    return jnp.sum(jnp.where(iota((1, LANES), 1) == i, row, 0.0), axis=1, keepdims=True)
+def sum_rows(rows):
+    while len(rows) > 1:
+        rows = [a + b for a, b in zip(rows[::2], rows[1::2])] + rows[len(rows) // 2 * 2 :]
+    return jnp.sum(rows[0], axis=1, keepdims=True)
 
 
 def middle_kernel(
@@ -365,10 +358,11 @@
             second = second + p * q
     out[...] = jnp.zeros(out.shape, F32)
     put_values(out, tab, own, inc, lst, ratio, shifted)
-    row = scalar_row([first, second])
     rows = 2 * CAP * street_size
-    for j in range(out.shape[0]):
-        out[j, rows] = row
+    for i, value in enumerate((first, second)):
+        row = jnp.sum(value, axis=0, keepdims=True)
+        for j in range(out.shape[0]):
+            out[j, rows + i] = row
 
 
 def dots_kernel(tab, grad, diag, direction, image, values, sent, got, resid, precond, steps, out):
@@ -376,11 +370,8 @@
     street_size = values.shape[0] // drives
     at = read_places(tab, street_size, drives * MATCH)
     rows = 2 * CAP * street_size
-    total = got[0, rows]
-    for j in range(1, got.shape[0]):
-        total = total + got[j, rows]
-    inner = pick_lane(total, 0)
-    curve = pick_lane(total, 1)
+    inner = sum_rows([got[j, rows] for j in range(got.shape[0])])
+    curve = sum_rows([got[j, rows + 1] for j in range(got.shape[0])])
     alpha = inner / curve
     one = jnp.zeros((SUB, LANES), F32)
     two = jnp.zeros((SUB, LANES), F32)
@@ -405,9 +396,10 @@
     head = iota((SUB, LANES), 0) == 0
     two = two + jnp.where(head, jnp.broadcast_to(slots2, (SUB, LANES)), 0.0)
     three = three + jnp.where(head, jnp.broadcast_to(slots3, (SUB, LANES)), 0.0)
-    row = scalar_row([one, two, three])
-    for j in range(out.shape[0]):
-        out[j] = row
+    for i, value in enumerate((one, two, three)):
+        row = jnp.sum(value, axis=0, keepdims=True)
+        for j in range(out.shape[0]):
+            out[j, i] = row
     lane = iota((SUB, LANES), 1)
     steps[...] = jnp.where(lane == 0, alpha, jnp.where(lane == 1, inner, curve))
 
@@ -469,15 +461,14 @@
 
 
 def finish_kernel(steps, got, o_p, o_z, o_r, o_h, o_q, step_out, resid_out):
-    total = got[0]
-    for j in range(1, got.shape[0]):
-        total = total + got[j]
-    inner_next = pick_lane(total, 0)
+    inner_next, second, third = (
+        sum_rows([got[j, i] for j in range(got.shape[0])]) for i in range(3)
+    )
     alpha = steps[0:1, 0:1]
     inner = steps[0:1, 1:2]
     curve = steps[0:1, 2:3]
     beta = inner_next / inner
-    denominator = pick_lane(total, 1) + 2.0 * beta * pick_lane(total, 2) + beta * beta * curve
+    denominator = second + 2.0 * beta * third + beta * beta * curve
     last = inner_next / denominator
     for a in range(o_p.shape[0]):
         p = o_p[a]
@@ -542,7 +533,7 @@
         send.reshape(blocks, 5, 4, LANES), ("drive", "street"), split_axis=0, concat_axis=0, tiled=True
     )
     exchange = ((lanes, 2 * CAP * street_size, 1, LANES), F32)
-    exchange2 = ((lanes, 2 * CAP * street_size + 1, 1, LANES), F32)
+    exchange2 = ((lanes, 2 * CAP * street_size + 2, 1, LANES), F32)
     acc = pltpu.VMEM((drives, 128, LANES), F32)
     shifted = pltpu.VMEM((drives, 4, HIGH, SUB, LANES), F32)
     list_size = CAP * blocks + UNROLL
@@ -574,7 +565,7 @@
     got2 = lax.all_to_all(sent2, "drive", split_axis=0, concat_axis=0, tiled=True)
     resid, precond, steps, sent3 = call(
         dots_kernel,
-        [param, param, ((SUB, LANES), F32), ((lanes, 1, LANES), F32)],
+        [param, param, ((SUB, LANES), F32), ((lanes, 3, 1, LANES), F32)],
         "svvvvvvv",
         "vvvv",
         name="dots",

time: 60.6 us -> 60.8 us (level)
  no operation moved by 1% of the time
where the time goes in v6:
time: 60.8 us; the launch traced here: 60.7 us
  blocking collectives  20.1 us (33%)
  Pallas kernels  14.2 us (23%)
  waiting for transfers between devices  13.1 us (22%)
  starting transfers between devices  12.6 us (21%)
  between operations  0.72 us (1%)
    all_to_all x1, blocking collectives, body(): got = lax.all_to_all(sent, 'drive', split_axis=0, concat_axis=0, tiled=True)  10.4 us
    all_to_all x1, blocking collectives, body(): lax.all_to_all(sent2, 'drive', split_axis=0, concat_axis=0, tiled=True)  9.73 us
    all_to_all x1, starting transfers between devices, body(): lax.all_to_all(send.reshape(blocks, 5, 4, LANES), ('drive', 'street'), sp...  7.3 us
    all_to_all x1, waiting for transfers between devices, body(): lax.all_to_all(send.reshape(blocks, 5, 4, LANES), ('drive', 'street'), sp...  6.09 us
    pallas_call x1, Pallas kernels, body(): call(start_kernel, [param, param, param, exchange, ((list_size,), jnp.int...  3.75 us
    all_to_all x1, waiting for transfers between devices, body(): lax.all_to_all(sent3, 'drive', split_axis=0, concat_axis=0, tiled=True)  3.7 us
    all_to_all x1, starting transfers between devices, body(): lax.all_to_all(sent3, 'drive', split_axis=0, concat_axis=0, tiled=True)  3.5 us
    ppermute x1, waiting for transfers between devices, body(): peer = lax.ppermute(mine, 'street', [(0, 1), (1, 0)])  3.3 us
  transfers between devices with their start and end apart: 3, of which 3 were waited for; matrix products, arithmetic and copies ran while one was open for 0% of the time, Pallas kernels for 5%

profile of v6, /device:TPU:0, one launch (start us, length us, event | category | flops | bytes accessed | tf_op | source)
XLA Modules:
  0.0 60.7 jit_solution(17434060305813802044)
XLA Ops:
  0.6 1.9 %send.1 = (f32[16,2,5,4,128]{4,3,2,1,0:T(4,128)}, f32[4,16,128]{2,1,0:T(8,128)}, s32[33]{0:T(128)}) custom-call(s32[4]{0:T(128)} %counts.1, s32[4,64]{1,0:T(4,128)} %bitcast.8, s32[4,64]{1,0:T(4,128)} %bitcast.9, s32[4,128]{1,0:T(4,128)} %knot_own.1, s32[4,128]{1,0:T(4,128)} %knot_par.1, s32[4,128]{1,0:T(4,128)} %match.1, f32[2,4,128]{2,1,0:T(4,128)} %spline.1, ...), custom_call_target="tpu_custom_call" | custom-call | tf_op jit(solution)/shard_map/send/pallas_call | solution.py:514
  2.5 0.0 copy-start.1
  2.5 7.3 %all-to-all-start = ((f32[32,5,4,128]{3,2,1,0:T(4,128)}), f32[32,5,4,128]{3,2,1,0:T(4,128)S(1)}, u32[]{:S(2)}, u32[]{:S(2)}) async-start(f32[32,5,4,128]{3,2,1,0:T(4,128)} %bitcast.7), calls=%async_computation | async-start | bytes 655360 | tf_op jit(solution)/shard_map/all_to_all | solution.py:532
  9.8 0.0 copy-done.1
  9.8 1.8 %collective-permute-start = (f32[4,16,128]{2,1,0:T(8,128)S(1)}, f32[4,16,128]{2,1,0:T(8,128)S(1)}, u32[]{:S(2)}, u32[]{:S(2)}) collective-permute-start(f32[4,16,128]{2,1,0:T(8,128)S(1)} %copy-done.1), channel_id=1, source_target_pairs={{0,1},{1,0},{2,3},{3,2},{4,5},{5,4},{6,7},{7,6},{8,9},{9,8},{10,11... | collective-permute-start | bytes 98312 | tf_op jit(solution)/shard_map/ppermute | solution.py:527
  11.7 3.3 %collective-permute-done = f32[4,16,128]{2,1,0:T(8,128)S(1)} collective-permute-done((f32[4,16,128]{2,1,0:T(8,128)S(1)}, f32[4,16,128]{2,1,0:T(8,128)S(1)}, u32[]{:S(2)}, u32[]{:S(2)}) %collective-permute-start) | collective-permute-done | bytes 32800 | tf_op jit(solution)/shard_map/ppermute | solution.py:527
  15.0 0.4 own.1.begun
  15.4 0.0 copy-start
  15.4 6.1 %all-to-all-done.inc = f32[32,5,4,128]{3,2,1,0:T(4,128)S(1)} async-done(((f32[32,5,4,128]{3,2,1,0:T(4,128)}), f32[32,5,4,128]{3,2,1,0:T(4,128)S(1)}, u32[]{:S(2)}, u32[]{:S(2)}) %all-to-all-start) | async-done | bytes 327712 | tf_op jit(solution)/shard_map/all_to_all | solution.py:532
  21.5 0.0 copy-done
  21.5 3.7 %start.1 = (f32[4,4,8,128]{3,2,1,0:T(8,128)S(1)}, f32[4,4,8,128]{3,2,1,0:T(8,128)S(1)}, f32[4,4,8,128]{3,2,1,0:T(8,128)S(1)}, f32[16,8,1,128]{3,2,1,0:T(1,128)S(1)}, s32[77]{0:T(128)S(1)}) custom-call(s32[33]{0:T(128)S(1)} %copy-done, f32[2,4,16,128]{3,2,1,0:T(8,128)S(1)} %pad_maximum_fusion.own, f32[32,5,4,128]{3,2,1,0:T(4,128)S(1)} %all-to-all-done.inc, ...), custom_call_target="tpu_custom_call" | custom-call | tf_op jit(solution)/shard_map/start/pallas_call | solution.py:548
  25.3 10.4 %all_to_all.20.got = f32[16,8,1,128]{3,2,1,0:T(1,128)S(1)} all-to-all(f32[16,8,1,128]{3,2,1,0:T(1,128)S(1)} %get-tuple-element.29.sent), channel_id=1, replica_groups=mesh['region'=1,'drive'=16,'street'=2] {'drive'}, dimensions={0} | all-to-all | bytes 131072 | tf_op jit(solution)/shard_map/all_to_all | solution.py:556
  35.7 3.2 %middle.1 = (f32[4,4,8,128]{3,2,1,0:T(8,128)S(1)}, f32[8,128]{1,0:T(8,128)S(1)}, f32[16,10,1,128]{3,2,1,0:T(1,128)S(1)}) custom-call(s32[33]{0:T(128)S(1)} %copy-done, s32[77]{0:T(128)S(1)} %get-tuple-element.28.lst, f32[2,4,16,128]{3,2,1,0:T(8,128)S(1)} %pad_maximum_fusion.own, f32[32,5,4,128]{3,2,1,0:T(4,128)S(1)} %all-to-all-done.inc, ...), custom_call_target="tpu_custom_call" | custom-call | tf_op jit(solution)/shard_map/middle/pallas_call | solution.py:557
  38.9 9.7 %all_to_all.21.got.got2 = f32[16,10,1,128]{3,2,1,0:T(1,128)S(1)} all-to-all(f32[16,10,1,128]{3,2,1,0:T(1,128)S(1)} %get-tuple-element.32.sent.sent2), channel_id=1, replica_groups=mesh['region'=1,'drive'=16,'street'=2] {'drive'}, dimensions={0} | all-to-all | bytes 163840 | tf_op jit(solution)/shard_map/all_to_all | solution.py:565
  48.6 1.3 %dots.1 = (f32[4,4,8,128]{3,2,1,0:T(8,128)S(1)}, f32[4,4,8,128]{3,2,1,0:T(8,128)S(1)}, f32[8,128]{1,0:T(8,128)S(1)}, f32[16,3,1,128]{3,2,1,0:T(1,128)}) custom-call(s32[33]{0:T(128)S(1)} %copy-done, f32[4,4,8,128]{3,2,1,0:T(8,128)S(1)} %get-tuple-element.25.grad, f32[4,4,8,128]{3,2,1,0:T(8,128)S(1)} %get-tuple-element.26.diag, ...), custom_call_target="tpu_custom_call" | custom-call | tf_op jit(solution)/shard_map/dots/pallas_call | solution.py:566
  49.9 3.5 %all-to-all-start.3 = ((f32[16,3,1,128]{3,2,1,0:T(1,128)}), f32[16,3,1,128]{3,2,1,0:T(1,128)S(1)}, u32[]{:S(2)}, u32[]{:S(2)}) async-start(f32[16,3,1,128]{3,2,1,0:T(1,128)} %get-tuple-element.34), calls=%async_computation.3 | async-start | bytes 49152 | tf_op jit(solution)/shard_map/all_to_all | solution.py:573
  53.4 2.8 %last.1 = (f32[4,4,384]{2,1,0:T(4,128)S(1)}, f32[4,4,384]{2,1,0:T(4,128)S(1)}, f32[4,4,384]{2,1,0:T(4,128)S(1)}, f32[4,4,384]{2,1,0:T(4,128)S(1)}, f32[4,4,384]{2,1,0:T(4,128)S(1)}) custom-call(s32[33]{0:T(128)S(1)} %copy-done, s32[77]{0:T(128)S(1)} %get-tuple-element.28.lst, f32[2,4,16,128]{3,2,1,0:T(8,128)S(1)} %pad_maximum_fusion.own, ...), custom_call_target="tpu_custom_call" | custom-call | flops 200000000 | bytes 8000000 | tf_op jit(solution)/shard_map/last/pallas_call | solution.py:575
  56.2 3.7 %all-to-all-done.3.got = f32[16,3,1,128]{3,2,1,0:T(1,128)S(1)} async-done(((f32[16,3,1,128]{3,2,1,0:T(1,128)}), f32[16,3,1,128]{3,2,1,0:T(1,128)S(1)}, u32[]{:S(2)}, u32[]{:S(2)}) %all-to-all-start.3) | async-done | bytes 24608 | tf_op jit(solution)/shard_map/all_to_all | solution.py:573
  59.9 0.8 %finish.1 = (f32[4,4,384]{2,1,0:T(4,128)}, f32[4,4,384]{2,1,0:T(4,128)}) custom-call(f32[8,128]{1,0:T(8,128)S(1)} %get-tuple-element.33.steps, f32[16,3,1,128]{3,2,1,0:T(1,128)S(1)} %all-to-all-done.3.got, f32[4,4,384]{2,1,0:T(4,128)S(1)} %get-tuple-element.37.o_p, f32[4,4,384]{2,1,0:T(4,128)S(1)} %get-tuple-element.38.o_z, ...), custom_call_target="tpu_custom_call" | custom-call | tf_op jit(solution)/shard_map/finish/pallas_call | solution.py:585
  (2 shorter events, 0.0 us)
Async XLA Ops:
  2.5 7.3 %copy-start.1 = (f32[4,16,128]{2,1,0:T(8,128)S(1)}, f32[4,16,128]{2,1,0:T(8,128)}, u32[]{:S(2)}) copy-start(f32[4,16,128]{2,1,0:T(8,128)} %get-tuple-element.23) | copy-start | bytes 98308
  2.5 19.0 %all-to-all-start = ((f32[32,5,4,128]{3,2,1,0:T(4,128)}), f32[32,5,4,128]{3,2,1,0:T(4,128)S(1)}, u32[]{:S(2)}, u32[]{:S(2)}) async-start(f32[32,5,4,128]{3,2,1,0:T(4,128)} %bitcast.7), calls=%async_computation | async-start | bytes 655360 | tf_op jit(solution)/shard_map/all_to_all | solution.py:532
  9.8 5.1 %collective-permute-start = (f32[4,16,128]{2,1,0:T(8,128)S(1)}, f32[4,16,128]{2,1,0:T(8,128)S(1)}, u32[]{:S(2)}, u32[]{:S(2)}) collective-permute-start(f32[4,16,128]{2,1,0:T(8,128)S(1)} %copy-done.1), channel_id=1, source_target_pairs={{0,1},{1,0},{2,3},{3,2},{4,5},{5,4},{6,7},{7,6},{8,9},{9,8},{10,11... | collective-permute-start | bytes 98312 | tf_op jit(solution)/shard_map/ppermute | solution.py:527
  15.4 6.1 %copy-start = (s32[33]{0:T(128)S(1)}, s32[33]{0:T(128)}, u32[]{:S(2)}) copy-start(s32[33]{0:T(128)} %get-tuple-element.22.tab) | copy-start | bytes 400
  49.9 10.0 %all-to-all-start.3 = ((f32[16,3,1,128]{3,2,1,0:T(1,128)}), f32[16,3,1,128]{3,2,1,0:T(1,128)S(1)}, u32[]{:S(2)}, u32[]{:S(2)}) async-start(f32[16,3,1,128]{3,2,1,0:T(1,128)} %get-tuple-element.34), calls=%async_computation.3 | async-start | bytes 49152 | tf_op jit(solution)/shard_map/all_to_all | solution.py:573

commit v7 on v6

--- a/solution.py
+++ b/solution.py
@@ -13,7 +13,7 @@
 HIGH = 4
 CAP = 2
 SUB = 8
-UNROLL = 13
+UNROLL = 14
 F32 = jnp.float32
 BF16 = jnp.bfloat16
 

time: 60.8 us -> 60.8 us (level)
  transfers between devices with their start and end apart: 3 -> 3, of which waited for: 3 -> 3; matrix products, arithmetic and copies ran while one was open for 0% -> 0% of each run, Pallas kernels for 5% -> 6%
where the time goes in v7:
time: 60.8 us; the launch traced here: 60.5 us
  blocking collectives  19.6 us (32%)
  Pallas kernels  14.5 us (24%)
  waiting for transfers between devices  13 us (21%)
  starting transfers between devices  12.6 us (21%)
  between operations  0.72 us (1%)
    all_to_all x1, blocking collectives, body(): got = lax.all_to_all(sent, 'drive', split_axis=0, concat_axis=0, tiled=True)  9.88 us
    all_to_all x1, blocking collectives, body(): lax.all_to_all(sent2, 'drive', split_axis=0, concat_axis=0, tiled=True)  9.73 us
    all_to_all x1, starting transfers between devices, body(): lax.all_to_all(send.reshape(blocks, 5, 4, LANES), ('drive', 'street'), sp...  7.3 us
    all_to_all x1, waiting for transfers between devices, body(): lax.all_to_all(send.reshape(blocks, 5, 4, LANES), ('drive', 'street'), sp...  6.09 us
    pallas_call x1, Pallas kernels, body(): call(start_kernel, [param, param, param, exchange, ((list_size,), jnp.int...  3.85 us
    all_to_all x1, waiting for transfers between devices, body(): lax.all_to_all(sent3, 'drive', split_axis=0, concat_axis=0, tiled=True)  3.57 us
    all_to_all x1, starting transfers between devices, body(): lax.all_to_all(sent3, 'drive', split_axis=0, concat_axis=0, tiled=True)  3.5 us
    ppermute x1, waiting for transfers between devices, body(): peer = lax.ppermute(mine, 'street', [(0, 1), (1, 0)])  3.3 us
  transfers between devices with their start and end apart: 3, of which 3 were waited for; matrix products, arithmetic and copies ran while one was open for 0% of the time, Pallas kernels for 6%

profile of v7, /device:TPU:0, one launch (start us, length us, event | category | flops | bytes accessed | tf_op | source)
XLA Modules:
  0.0 60.5 jit_solution(17421355042683851151)
XLA Ops:
  0.6 1.9 %send.1 = (f32[16,2,5,4,128]{4,3,2,1,0:T(4,128)}, f32[4,16,128]{2,1,0:T(8,128)}, s32[33]{0:T(128)}) custom-call(s32[4]{0:T(128)} %counts.1, s32[4,64]{1,0:T(4,128)} %bitcast.8, s32[4,64]{1,0:T(4,128)} %bitcast.9, s32[4,128]{1,0:T(4,128)} %knot_own.1, s32[4,128]{1,0:T(4,128)} %knot_par.1, s32[4,128]{1,0:T(4,128)} %match.1, f32[2,4,128]{2,1,0:T(4,128)} %spline.1, ...), custom_call_target="tpu_custom_call" | custom-call | tf_op jit(solution)/shard_map/send/pallas_call | solution.py:514
  2.5 0.0 copy-start.1
  2.5 7.3 %all-to-all-start = ((f32[32,5,4,128]{3,2,1,0:T(4,128)}), f32[32,5,4,128]{3,2,1,0:T(4,128)S(1)}, u32[]{:S(2)}, u32[]{:S(2)}) async-start(f32[32,5,4,128]{3,2,1,0:T(4,128)} %bitcast.7), calls=%async_computation | async-start | bytes 655360 | tf_op jit(solution)/shard_map/all_to_all | solution.py:532
  9.8 0.0 copy-done.1
  9.8 1.8 %collective-permute-start = (f32[4,16,128]{2,1,0:T(8,128)S(1)}, f32[4,16,128]{2,1,0:T(8,128)S(1)}, u32[]{:S(2)}, u32[]{:S(2)}) collective-permute-start(f32[4,16,128]{2,1,0:T(8,128)S(1)} %copy-done.1), channel_id=1, source_target_pairs={{0,1},{1,0},{2,3},{3,2},{4,5},{5,4},{6,7},{7,6},{8,9},{9,8},{10,11... | collective-permute-start | bytes 98312 | tf_op jit(solution)/shard_map/ppermute | solution.py:527
  11.7 3.3 %collective-permute-done = f32[4,16,128]{2,1,0:T(8,128)S(1)} collective-permute-done((f32[4,16,128]{2,1,0:T(8,128)S(1)}, f32[4,16,128]{2,1,0:T(8,128)S(1)}, u32[]{:S(2)}, u32[]{:S(2)}) %collective-permute-start) | collective-permute-done | bytes 32800 | tf_op jit(solution)/shard_map/ppermute | solution.py:527
  15.0 0.4 own.1.begun
  15.4 0.0 copy-start
  15.4 6.1 %all-to-all-done.inc = f32[32,5,4,128]{3,2,1,0:T(4,128)S(1)} async-done(((f32[32,5,4,128]{3,2,1,0:T(4,128)}), f32[32,5,4,128]{3,2,1,0:T(4,128)S(1)}, u32[]{:S(2)}, u32[]{:S(2)}) %all-to-all-start) | async-done | bytes 327712 | tf_op jit(solution)/shard_map/all_to_all | solution.py:532
  21.5 0.0 copy-done
  21.5 3.9 %start.1 = (f32[4,4,8,128]{3,2,1,0:T(8,128)S(1)}, f32[4,4,8,128]{3,2,1,0:T(8,128)S(1)}, f32[4,4,8,128]{3,2,1,0:T(8,128)S(1)}, f32[16,8,1,128]{3,2,1,0:T(1,128)S(1)}, s32[78]{0:T(128)S(1)}) custom-call(s32[33]{0:T(128)S(1)} %copy-done, f32[2,4,16,128]{3,2,1,0:T(8,128)S(1)} %pad_maximum_fusion.own, f32[32,5,4,128]{3,2,1,0:T(4,128)S(1)} %all-to-all-done.inc, ...), custom_call_target="tpu_custom_call" | custom-call | tf_op jit(solution)/shard_map/start/pallas_call | solution.py:548
  25.4 9.9 %all_to_all.20.got = f32[16,8,1,128]{3,2,1,0:T(1,128)S(1)} all-to-all(f32[16,8,1,128]{3,2,1,0:T(1,128)S(1)} %get-tuple-element.29.sent), channel_id=1, replica_groups=mesh['region'=1,'drive'=16,'street'=2] {'drive'}, dimensions={0} | all-to-all | bytes 131072 | tf_op jit(solution)/shard_map/all_to_all | solution.py:556
  35.3 3.3 %middle.1 = (f32[4,4,8,128]{3,2,1,0:T(8,128)S(1)}, f32[8,128]{1,0:T(8,128)S(1)}, f32[16,10,1,128]{3,2,1,0:T(1,128)S(1)}) custom-call(s32[33]{0:T(128)S(1)} %copy-done, s32[78]{0:T(128)S(1)} %get-tuple-element.28.lst, f32[2,4,16,128]{3,2,1,0:T(8,128)S(1)} %pad_maximum_fusion.own, f32[32,5,4,128]{3,2,1,0:T(4,128)S(1)} %all-to-all-done.inc, ...), custom_call_target="tpu_custom_call" | custom-call | tf_op jit(solution)/shard_map/middle/pallas_call | solution.py:557
  38.6 9.7 %all_to_all.21.got.got2 = f32[16,10,1,128]{3,2,1,0:T(1,128)S(1)} all-to-all(f32[16,10,1,128]{3,2,1,0:T(1,128)S(1)} %get-tuple-element.32.sent.sent2), channel_id=1, replica_groups=mesh['region'=1,'drive'=16,'street'=2] {'drive'}, dimensions={0} | all-to-all | bytes 163840 | tf_op jit(solution)/shard_map/all_to_all | solution.py:565
  48.3 1.3 %dots.1 = (f32[4,4,8,128]{3,2,1,0:T(8,128)S(1)}, f32[4,4,8,128]{3,2,1,0:T(8,128)S(1)}, f32[8,128]{1,0:T(8,128)S(1)}, f32[16,3,1,128]{3,2,1,0:T(1,128)}) custom-call(s32[33]{0:T(128)S(1)} %copy-done, f32[4,4,8,128]{3,2,1,0:T(8,128)S(1)} %get-tuple-element.25.grad, f32[4,4,8,128]{3,2,1,0:T(8,128)S(1)} %get-tuple-element.26.diag, ...), custom_call_target="tpu_custom_call" | custom-call | tf_op jit(solution)/shard_map/dots/pallas_call | solution.py:566
  49.6 3.5 %all-to-all-start.3 = ((f32[16,3,1,128]{3,2,1,0:T(1,128)}), f32[16,3,1,128]{3,2,1,0:T(1,128)S(1)}, u32[]{:S(2)}, u32[]{:S(2)}) async-start(f32[16,3,1,128]{3,2,1,0:T(1,128)} %get-tuple-element.34), calls=%async_computation.3 | async-start | bytes 49152 | tf_op jit(solution)/shard_map/all_to_all | solution.py:573
  53.1 3.0 %last.1 = (f32[4,4,384]{2,1,0:T(4,128)S(1)}, f32[4,4,384]{2,1,0:T(4,128)S(1)}, f32[4,4,384]{2,1,0:T(4,128)S(1)}, f32[4,4,384]{2,1,0:T(4,128)S(1)}, f32[4,4,384]{2,1,0:T(4,128)S(1)}) custom-call(s32[33]{0:T(128)S(1)} %copy-done, s32[78]{0:T(128)S(1)} %get-tuple-element.28.lst, f32[2,4,16,128]{3,2,1,0:T(8,128)S(1)} %pad_maximum_fusion.own, ...), custom_call_target="tpu_custom_call" | custom-call | flops 200000000 | bytes 8000000 | tf_op jit(solution)/shard_map/last/pallas_call | solution.py:575
  56.1 3.6 %all-to-all-done.3.got = f32[16,3,1,128]{3,2,1,0:T(1,128)S(1)} async-done(((f32[16,3,1,128]{3,2,1,0:T(1,128)}), f32[16,3,1,128]{3,2,1,0:T(1,128)S(1)}, u32[]{:S(2)}, u32[]{:S(2)}) %all-to-all-start.3) | async-done | bytes 24608 | tf_op jit(solution)/shard_map/all_to_all | solution.py:573
  59.6 0.8 %finish.1 = (f32[4,4,384]{2,1,0:T(4,128)}, f32[4,4,384]{2,1,0:T(4,128)}) custom-call(f32[8,128]{1,0:T(8,128)S(1)} %get-tuple-element.33.steps, f32[16,3,1,128]{3,2,1,0:T(1,128)S(1)} %all-to-all-done.3.got, f32[4,4,384]{2,1,0:T(4,128)S(1)} %get-tuple-element.37.o_p, f32[4,4,384]{2,1,0:T(4,128)S(1)} %get-tuple-element.38.o_z, ...), custom_call_target="tpu_custom_call" | custom-call | tf_op jit(solution)/shard_map/finish/pallas_call | solution.py:585
  (2 shorter events, 0.0 us)
Async XLA Ops:
  2.5 7.3 %copy-start.1 = (f32[4,16,128]{2,1,0:T(8,128)S(1)}, f32[4,16,128]{2,1,0:T(8,128)}, u32[]{:S(2)}) copy-start(f32[4,16,128]{2,1,0:T(8,128)} %get-tuple-element.23) | copy-start | bytes 98308
  2.5 19.0 %all-to-all-start = ((f32[32,5,4,128]{3,2,1,0:T(4,128)}), f32[32,5,4,128]{3,2,1,0:T(4,128)S(1)}, u32[]{:S(2)}, u32[]{:S(2)}) async-start(f32[32,5,4,128]{3,2,1,0:T(4,128)} %bitcast.7), calls=%async_computation | async-start | bytes 655360 | tf_op jit(solution)/shard_map/all_to_all | solution.py:532
  9.8 5.1 %collective-permute-start = (f32[4,16,128]{2,1,0:T(8,128)S(1)}, f32[4,16,128]{2,1,0:T(8,128)S(1)}, u32[]{:S(2)}, u32[]{:S(2)}) collective-permute-start(f32[4,16,128]{2,1,0:T(8,128)S(1)} %copy-done.1), channel_id=1, source_target_pairs={{0,1},{1,0},{2,3},{3,2},{4,5},{5,4},{6,7},{7,6},{8,9},{9,8},{10,11... | collective-permute-start | bytes 98312 | tf_op jit(solution)/shard_map/ppermute | solution.py:527
  15.4 6.1 %copy-start = (s32[33]{0:T(128)S(1)}, s32[33]{0:T(128)}, u32[]{:S(2)}) copy-start(s32[33]{0:T(128)} %get-tuple-element.22.tab) | copy-start | bytes 400
  49.6 10.0 %all-to-all-start.3 = ((f32[16,3,1,128]{3,2,1,0:T(1,128)}), f32[16,3,1,128]{3,2,1,0:T(1,128)S(1)}, u32[]{:S(2)}, u32[]{:S(2)}) async-start(f32[16,3,1,128]{3,2,1,0:T(1,128)} %get-tuple-element.34), calls=%async_computation.3 | async-start | bytes 49152 | tf_op jit(solution)/shard_map/all_to_all | solution.py:573
